TPU v7x, 256 devices: a whole 4x4x8 slice. The times are simulated.
256 devices in a mesh: rows: 32 (over z, y_lo, core), chan: 8 (over x, y_hi).
Axes of the slice: x: 4, y: 4 (y_hi: 2, y_lo: 2; y = y_hi * 2 + y_lo), z: 8, core: 2. Of those that a mesh axis runs over, the one named last changes fastest.
Arguments:
- frame_one: bfloat16 [8192, 256], P('rows', 'chan'), may hold values from -6 to 6
- frame_two: bfloat16 [256, 480, 256], P('rows', None, 'chan'), may hold values from -6 to 6
Outputs:
- pyramid: bfloat16 [32, 5040, 8192], P(None, 'chan', 'rows')
All inputs are finite; a program needn't handle non-finite values.
Results may differ from a plain program's by a relative error of at most 0.0016.
Values may be sent and summed in bfloat16 or wider, within the bound.
A program may use at most 128 MiB of HBM per device.

v0:
```python
import jax
import jax.numpy as jnp
from jax import lax
from jax.sharding import PartitionSpec as P


def pool_strip(strip):
    full = strip.astype(jnp.float32)
    rows_n, cols_n, chans = full.shape
    level_one = full.reshape(rows_n // 2, 2, cols_n // 2, 2, chans).mean(axis=(1, 3))
    level_two = level_one.reshape(rows_n // 4, 2, cols_n // 4, 2, chans).mean(axis=(1, 3))
    joined = jnp.concatenate(
        [full.reshape(-1, chans), level_one.reshape(-1, chans), level_two.reshape(-1, chans)],
        axis=0,
    )
    return joined.astype(jnp.bfloat16)


def local(frame_one, frame_two):
    queries = lax.all_gather(frame_one, "chan", axis=1, tiled=True)
    channels = queries.shape[1]
    factor = 1.0 / jnp.sqrt(jnp.float32(channels))
    pooled = pool_strip(frame_two)
    strip_count = lax.axis_size("rows")
    groups = lax.axis_size("chan")
    share = pooled.shape[0] // groups
    slices = pooled.shape[1]
    arranged = jnp.transpose(pooled.reshape(groups, share, slices), (0, 2, 1))
    gathered = lax.all_gather(arranged, "rows", axis=1, tiled=True)
    traded = lax.all_to_all(gathered, "chan", split_axis=0, concat_axis=1, tiled=True)
    traded = traded.reshape(groups, strip_count, slices, share)
    split_queries = queries.reshape(queries.shape[0], groups, slices)
    values = jnp.einsum("kscp,qkc->spq", traded, split_queries, preferred_element_type=jnp.float32)
    return (values * factor).astype(jnp.bfloat16)


def solution(mesh):
    in_specs = (P("rows", "chan"), P("rows", None, "chan"))
    out_specs = P(None, "chan", "rows")
    return jax.shard_map(local, mesh=mesh, in_specs=in_specs, out_specs=out_specs, check_vma=False)
```

profile of v0, /device:TPU:8, one launch (start us, length us, event | category | flops | bytes accessed | tf_op | source)
XLA Modules:
  0.0 323.0 jit_solution(6841564967773849666)
XLA Ops:
  6.5 0.0 all-gather.2.cloned.1.call-start
  6.5 1.1 copy.14
  7.6 1.3 copy.15
  8.9 0.4 reshape.37
  9.3 1.6 reduce_sum.18
  10.9 0.1 broadcast_multiply_fusion
  11.0 0.4 reduce_sum.19
  11.4 0.1 copy.17
  11.5 0.1 copy.22
  11.6 0.1 concatenate.4
  11.7 1.2 convert_element_type.9
  12.9 0.0 all-gather.2.cloned.1.call-update
  12.9 77.6 %all-gather.2.cloned.1.call-done = bf16[8,1024,630]{2,0,1:T(8,128)(2,1)} async-done(((bf16[8,32,630]{2,0,1:T(8,128)(2,1)}), bf16[8,1024,630]{2,0,1:T(8,128)(2,1)}) %all-gather.2.cloned.1.call-update) | async-done | bytes 10321936 | tf_op jit(solution)/shard_map/all_gather | solution.py:29
  90.5 15.1 %copy.18 = bf16[8,1024,630]{1,2,0:T(8,128)(2,1)} copy(bf16[8,1024,630]{2,0,1:T(8,128)(2,1)} %all-gather.2.cloned.1.call-done) | data formatting | bytes 20643840 | tf_op jit(solution)/shard_map/all_gather | solution.py:29
  105.6 0.0 copy-start
  105.6 6.0 %all-to-all-start = ((bf16[8,1024,630]{1,2,0:T(8,128)(2,1)}), bf16[8,1024,630]{1,2,0:T(8,128)(2,1)}, u32[]{:S(2)}, u32[]{:S(2)}) async-start(bf16[8,1024,630]{1,2,0:T(8,128)(2,1)} %copy.18), calls=%async_computation | async-start | bytes 20709376 | tf_op jit(solution)/shard_map/all_to_all | solution.py:30
  111.6 0.0 copy-done
  111.6 168.7 %all_gather.7 = bf16[256,256]{0,1:T(8,128)(2,1)S(1)} all-gather(bf16[256,32]{0,1:T(8,128)(2,1)S(1)} %copy-done), channel_id=1, replica_groups=mesh['rows'=32,'chan'=8] {'chan'}, dimensions={1}, use_global_device_ids=true | all-gather | bytes 147456 | tf_op jit(solution)/shard_map/all_gather | solution.py:20
  280.3 0.0 all-to-all-done
  280.3 14.6 %copy.19 = bf16[8,1024,630]{2,1,0:T(8,128)(2,1)} copy(bf16[8,1024,630]{1,2,0:T(8,128)(2,1)} %all-to-all-done) | data formatting | bytes 20643840 | tf_op jit(solution)/shard_map/all_to_all | solution.py:30
  294.9 10.7 %fusion = bf16[32,630,256]{2,1,0:T(8,128)(2,1)} fusion(bf16[8,32,32,630]{3,2,1,0:T(8,128)(2,1)} %bitcast.21, bf16[256,8,32,1]{0,2,3,1:T(8,128)(2,1)S(1)} %bitcast.27), kind=kOutput, calls=%fused_computation.1 | convolution fusion | flops 2652733440 | bytes 20774912 | tf_op jit(solution)/shard_map/kscp,qkc->spq/dot_general | solution.py:33
  305.6 10.5 %copy.20 = bf16[32,630,256]{2,0,1:T(8,128)(2,1)} copy(bf16[32,630,256]{2,1,0:T(8,128)(2,1)} %fusion) | data formatting | bytes 20643840 | tf_op jit(solution)/shard_map/convert_element_type | solution.py:34
  (1 shorter events, 0.0 us)
Async XLA Ops:
  6.5 84.0 %all-gather.2.cloned.1.call-start = ((), (), s32[]{:S(2)}) async-start(), calls=%async_computation.1 | async-start | bytes 10813440 | tf_op jit(solution)/shard_map/all_gather | solution.py:29
  105.6 6.0 %copy-start = (bf16[256,32]{0,1:T(8,128)(2,1)S(1)}, bf16[256,32]{0,1:T(8,128)(2,1)}, u32[]{:S(2)}) copy-start(bf16[256,32]{0,1:T(8,128)(2,1)} %param.2) | copy-start | bytes 49156
  105.6 174.7 %all-to-all-start = ((bf16[8,1024,630]{1,2,0:T(8,128)(2,1)}), bf16[8,1024,630]{1,2,0:T(8,128)(2,1)}, u32[]{:S(2)}, u32[]{:S(2)}) async-start(bf16[8,1024,630]{1,2,0:T(8,128)(2,1)} %copy.18), calls=%async_computation | async-start | bytes 20709376 | tf_op jit(solution)/shard_map/all_to_all | solution.py:30
Sparse Core Ops, SparseCore 0:
  13.0 77.4 all-gather.1
where the time goes:
time: 324 us; the launch traced here: 323 us
  blocking collectives  169 us (52%)
  waiting for transfers between devices  77.6 us (24%)
  local copies, waits for them, and re-layouts  44.4 us (14%)
  between operations  13.4 us (4%)
  matrix products  10.7 us (3%)
  starting transfers between devices  5.99 us (2%)
    all_gather x1, blocking collectives, local(): queries = lax.all_gather(frame_one, 'chan', axis=1, tiled=True)  169 us
    all_gather x1, waiting for transfers between devices, local(): gathered = lax.all_gather(arranged, 'rows', axis=1, tiled=True)  77.6 us
    all_gather x1, local copies, waits for them, and re-layouts, local(): gathered = lax.all_gather(arranged, 'rows', axis=1, tiled=True)  15.1 us
    all_to_all x1, local copies, waits for them, and re-layouts, local(): lax.all_to_all(gathered, 'chan', split_axis=0, concat_axis=1, tiled=True)  14.6 us
    dot_general x1, matrix products, local(): jnp.einsum('kscp,qkc->spq', traded, split_queries, preferred_element_type...  10.7 us
    convert_element_type x1, local copies, waits for them, and re-layouts, local(): return (values * factor).astype(jnp.bfloat16)  10.5 us
  transfers between devices with their start and end apart: 2, of which 1 were waited for; matrix products, arithmetic and copies ran while one was open for 0% of the time, Pallas kernels for 0%

commit v1 on v0

--- a/solution.py
+++ b/solution.py
@@ -21,17 +21,16 @@
     channels = queries.shape[1]
     factor = 1.0 / jnp.sqrt(jnp.float32(channels))
     pooled = pool_strip(frame_two)
-    strip_count = lax.axis_size("rows")
     groups = lax.axis_size("chan")
     share = pooled.shape[0] // groups
     slices = pooled.shape[1]
-    arranged = jnp.transpose(pooled.reshape(groups, share, slices), (0, 2, 1))
-    gathered = lax.all_gather(arranged, "rows", axis=1, tiled=True)
-    traded = lax.all_to_all(gathered, "chan", split_axis=0, concat_axis=1, tiled=True)
-    traded = traded.reshape(groups, strip_count, slices, share)
+    blocks = pooled.reshape(groups, share, slices)
+    traded = lax.all_to_all(blocks, "chan", split_axis=0, concat_axis=0, tiled=True)
+    gathered = lax.all_gather(traded, "rows", axis=0, tiled=False)
     split_queries = queries.reshape(queries.shape[0], groups, slices)
-    values = jnp.einsum("kscp,qkc->spq", traded, split_queries, preferred_element_type=jnp.float32)
-    return (values * factor).astype(jnp.bfloat16)
+    values = jnp.einsum("skpc,qkc->psq", gathered, split_queries, preferred_element_type=jnp.float32)
+    values = (values * factor).astype(jnp.bfloat16)
+    return jnp.transpose(values, (1, 0, 2))
 
 
 def solution(mesh):

time: 324 us -> 132 us (0.41)
  blocking collectives: 169 us -> 50.1 us
  waiting for transfers between devices: 77.6 us -> 40 us
  local copies, waits for them, and re-layouts: 44.4 us -> 14 us
  starting transfers between devices: 5.99 us -> 0.01 us
    all_gather x1, blocking collectives: 169 us -> 34.7 us  [local(): queries = lax.all_gather(frame_one, 'chan', axis=1, tiled=True)]
    all_gather x1, waiting for transfers between devices: 77.6 us -> 39.9 us  [local(): gathered = lax.all_gather(traded, 'rows', axis=0, tiled=False)]
    all_to_all x0 -> x1, blocking collectives: none -> 15.4 us  [local(): lax.all_to_all(blocks, 'chan', split_axis=0, concat_axis=0, tiled=True)]
    all_gather x1 -> x0, local copies, waits for them, and re-layouts: 15.1 us -> none  [local(): gathered = lax.all_gather(arranged, 'rows', axis=1, tiled=True)]
    all_to_all x1 -> x0, local copies, waits for them, and re-layouts: 14.6 us -> none  [local(): lax.all_to_all(gathered, 'chan', split_axis=0, concat_axis=1, tiled=True)]
    all_to_all x1 -> x0, starting transfers between devices: 5.99 us -> none  [local(): lax.all_to_all(gathered, 'chan', split_axis=0, concat_axis=1, tiled=True)]
  transfers between devices with their start and end apart: 2 -> 1, of which waited for: 1 -> 1; matrix products, arithmetic and copies ran while one was open for 0% -> 0% of each run, Pallas kernels for 0% -> 0%
where the time goes in v1:
time: 132 us; the launch traced here: 130 us
  blocking collectives  50.1 us (38%)
  waiting for transfers between devices  40 us (30%)
  local copies, waits for them, and re-layouts  14 us (11%)
  between operations  13.5 us (10%)
  matrix products  10.7 us (8%)
  other arithmetic  2.08 us (2%)
    all_gather x1, waiting for transfers between devices, local(): gathered = lax.all_gather(traded, 'rows', axis=0, tiled=False)  39.9 us
    all_gather x1, blocking collectives, local(): queries = lax.all_gather(frame_one, 'chan', axis=1, tiled=True)  34.7 us
    all_to_all x1, blocking collectives, local(): lax.all_to_all(blocks, 'chan', split_axis=0, concat_axis=0, tiled=True)  15.4 us
    dot_general x1, matrix products, local(): jnp.einsum('skpc,qkc->psq', gathered, split_queries, preferred_element_ty...  10.7 us
    convert_element_type x1, local copies, waits for them, and re-layouts, local(): values = (values * factor).astype(jnp.bfloat16)  10.5 us
  transfers between devices with their start and end apart: 1, of which 1 were waited for; matrix products, arithmetic and copies ran while one was open for 0% of the time, Pallas kernels for 0%

profile of v1, /device:TPU:8, one launch (start us, length us, event | category | flops | bytes accessed | tf_op | source)
XLA Modules:
  0.0 130.4 jit_solution(17889326251814811727)
XLA Ops:
  6.5 0.0 copy-start
  6.5 0.0 all-gather.3.cloned.1.call-start
  6.5 1.1 copy.19
  7.7 1.3 copy.20
  9.0 0.3 reshape.30
  9.3 1.6 %reduce_sum.18 = f32[4,240,32]{2,1,0:T(8,128)S(1)} reduce(f32[4,2,240,2,32]{4,3,2,1,0:T(2,128)S(1)} %bitcast.19, f32[]{:T(128)} %constant.3.clone.1), dimensions={1,3}, to_apply=%region_0.0 | reduce | flops 92160 | bytes 614404 | tf_op jit(solution)/shard_map/reduce_sum | solution.py:10
  10.9 0.1 broadcast_multiply_fusion
  11.0 0.4 reduce_sum.19
  11.4 0.1 copy.22
  11.5 0.1 copy.26
  11.6 0.1 concatenate.4
  11.7 0.4 convert_element_type.10
  12.2 15.4 %all_to_all.5 = bf16[8,630,32]{1,2,0:T(8,128)(2,1)} all-to-all(bf16[8,630,32]{1,2,0:T(8,128)(2,1)S(1)} %copy.23), channel_id=1, replica_groups=mesh['rows'=32,'chan'=8] {'chan'}, dimensions={0} | all-to-all | bytes 645120 | tf_op jit(solution)/shard_map/all_to_all | solution.py:28
  27.6 0.0 all-gather.3.cloned.1.call-update
  27.7 0.0 copy-done
  27.7 34.7 %all_gather.11 = bf16[256,256]{0,1:T(8,128)(2,1)S(1)} all-gather(bf16[256,32]{0,1:T(8,128)(2,1)S(1)} %copy-done), channel_id=1, replica_groups=mesh['rows'=32,'chan'=8] {'chan'}, dimensions={1}, use_global_device_ids=true | all-gather | bytes 147456 | tf_op jit(solution)/shard_map/all_gather | solution.py:20
  62.4 39.9 %all-gather.3.cloned.1.call-done = bf16[256,630,32]{1,2,0:T(8,128)(2,1)} async-done(((bf16[8,630,32]{1,2,0:T(8,128)(2,1)}), bf16[256,630,32]{1,2,0:T(8,128)(2,1)}) %all-gather.3.cloned.1.call-update) | async-done | bytes 10321936 | tf_op jit(solution)/shard_map/all_gather | solution.py:29
  102.3 10.7 %fusion = bf16[32,630,256]{2,1,0:T(8,128)(2,1)} fusion(bf16[32,8,630,32]{2,3,1,0:T(8,128)(2,1)} %bitcast.24, bf16[256,8,32,1]{0,2,1,3:T(8,128)(2,1)S(1)} %bitcast.23), kind=kOutput, calls=%fused_computation.1 | convolution fusion | flops 2652733440 | bytes 20774912 | tf_op jit(solution)/shard_map/skpc,qkc->psq/dot_general | solution.py:31
  113.0 10.5 %copy.24 = bf16[32,630,256]{2,0,1:T(8,128)(2,1)} copy(bf16[32,630,256]{2,1,0:T(8,128)(2,1)} %fusion) | data formatting | bytes 20643840 | tf_op jit(solution)/shard_map/convert_element_type | solution.py:32
  (2 shorter events, 0.1 us)
Async XLA Ops:
  6.5 21.1 %copy-start = (bf16[256,32]{0,1:T(8,128)(2,1)S(1)}, bf16[256,32]{0,1:T(8,128)(2,1)}, u32[]{:S(2)}) copy-start(bf16[256,32]{0,1:T(8,128)(2,1)} %param.2) | copy-start | bytes 49156
  6.5 95.8 %all-gather.3.cloned.1.call-start = ((), (), s32[]{:S(2)}) async-start(), calls=%async_computation.1 | async-start | bytes 10813440 | tf_op jit(solution)/shard_map/all_gather | solution.py:29
Sparse Core Ops, SparseCore 0:
  27.8 74.4 all-gather.2

commit v2 on v1

v2 whole, which is shorter than its diff:
```python
import jax
import jax.numpy as jnp
from jax import lax
from jax.sharding import Mesh, PartitionSpec as P


def pool_strip(strip):
    full = strip.astype(jnp.float32)
    rows_n, cols_n, chans = full.shape
    level_one = full.reshape(rows_n // 2, 2, cols_n // 2, 2, chans).mean(axis=(1, 3))
    level_two = level_one.reshape(rows_n // 4, 2, cols_n // 4, 2, chans).mean(axis=(1, 3))
    joined = jnp.concatenate(
        [full.reshape(-1, chans), level_one.reshape(-1, chans), level_two.reshape(-1, chans)],
        axis=0,
    )
    return joined.astype(jnp.bfloat16)


def local(frame_one, frame_two):
    queries = lax.all_gather(frame_one, "chan", axis=1, tiled=True)
    channels = queries.shape[1]
    factor = 1.0 / jnp.sqrt(jnp.float32(channels))
    pooled = pool_strip(frame_two)
    groups = lax.axis_size("chan")
    cores = lax.axis_size("core")
    share = pooled.shape[0] // groups
    slices = pooled.shape[1]
    blocks = pooled.reshape(groups, share, slices)
    traded = lax.all_to_all(blocks, "chan", split_axis=0, concat_axis=0, tiled=True)
    halves = traded.reshape(cores, groups // cores, share, slices)
    mine = lax.all_to_all(halves, "core", split_axis=0, concat_axis=0, tiled=True)
    gathered = lax.all_gather(mine, "grp", axis=0, tiled=False)
    both = lax.all_gather(gathered, "core", axis=0, tiled=False)
    split_queries = queries.reshape(queries.shape[0], cores, groups // cores, slices)
    values = jnp.einsum("hgrkpc,qhkc->pgrq", both, split_queries, preferred_element_type=jnp.float32)
    values = (values * factor).astype(jnp.bfloat16)
    values = values.reshape(share, -1, values.shape[-1])
    return jnp.transpose(values, (1, 0, 2))


def solution(mesh):
    rows = mesh.shape["rows"]
    devices = mesh.devices.reshape(rows // 2, 2, mesh.shape["chan"])
    fine = Mesh(devices, ("grp", "core", "chan"))
    strips = ("grp", "core")
    in_specs = (P(strips, "chan"), P(strips, None, "chan"))
    out_specs = P(None, "chan", strips)
    return jax.shard_map(local, mesh=fine, in_specs=in_specs, out_specs=out_specs, check_vma=False)
```

time: 132 us -> 232 us (1.76)
  waiting for transfers between devices: 40 us -> 119 us
  other arithmetic: 2.08 us -> 14.9 us
  blocking collectives: 50.1 us -> 53.5 us
  matrix products: 10.7 us -> 13.8 us
    all_gather x1 -> x2, waiting for transfers between devices: 39.9 us -> 119 us  [the longest x1 119 us: local(): gathered = lax.all_gather(mine, 'grp', axis=0, tiled=False)]
    convert_element_type x0 -> x1, other arithmetic: none -> 12.8 us  [local(): values = (values * factor).astype(jnp.bfloat16)]
    convert_element_type x1 -> x0, local copies, waits for them, and re-layouts: 10.5 us -> none  [local(): values = (values * factor).astype(jnp.bfloat16)]
    transpose x0 -> x1, local copies, waits for them, and re-layouts: none -> 10.5 us  [local(): return jnp.transpose(values, (1, 0, 2))]
    all_to_all x0 -> x1, blocking collectives: none -> 4 us  [local(): lax.all_to_all(halves, 'core', split_axis=0, concat_axis=0, tiled=True)]
    dot_general x1, matrix products: 10.7 us -> 13.8 us  [local(): jnp.einsum('hgrkpc,qhkc->pgrq', both, split_queries, preferred_element_ty...]
  transfers between devices with their start and end apart: 1 -> 2, of which waited for: 1 -> 1; matrix products, arithmetic and copies ran while one was open for 0% -> 0% of each run, Pallas kernels for 0% -> 0%
where the time goes in v2:
time: 232 us; the launch traced here: 230 us
  waiting for transfers between devices  119 us (51%)
  blocking collectives  53.5 us (23%)
  local copies, waits for them, and re-layouts  14.9 us (6%)
  other arithmetic  14.9 us (6%)
  matrix products  13.8 us (6%)
  between operations  13.5 us (6%)
    all_gather x1, waiting for transfers between devices, local(): gathered = lax.all_gather(mine, 'grp', axis=0, tiled=False)  119 us
    all_gather x1, blocking collectives, local(): queries = lax.all_gather(frame_one, 'chan', axis=1, tiled=True)  34.2 us
    all_to_all x1, blocking collectives, local(): lax.all_to_all(blocks, 'chan', split_axis=0, concat_axis=0, tiled=True)  15.3 us
    dot_general x1, matrix products, local(): jnp.einsum('hgrkpc,qhkc->pgrq', both, split_queries, preferred_element_ty...  13.8 us
    convert_element_type x1, other arithmetic, local(): values = (values * factor).astype(jnp.bfloat16)  12.8 us
    transpose x1, local copies, waits for them, and re-layouts, local(): return jnp.transpose(values, (1, 0, 2))  10.5 us
  transfers between devices with their start and end apart: 2, of which 1 were waited for; matrix products, arithmetic and copies ran while one was open for 0% of the time, Pallas kernels for 0%

profile of v2, /device:TPU:8, one launch (start us, length us, event | category | flops | bytes accessed | tf_op | source)
XLA Modules:
  0.0 230.0 jit_solution(2143590672033945344)
XLA Ops:
  6.5 0.0 copy-start
  6.5 0.0 all-gather.5.cloned.1.call-start
  6.5 1.1 copy.29
  7.7 1.3 copy.30
  9.0 0.3 reshape.36
  9.3 1.6 reduce_sum.18
  10.9 0.1 broadcast_multiply_fusion
  11.0 0.4 reduce_sum.19
  11.4 0.1 copy.32
  11.5 0.1 copy.40
  11.6 0.1 concatenate.4
  11.7 0.4 convert_element_type.12
  12.2 15.3 %all_to_all.10 = bf16[8,630,32]{1,2,0:T(8,128)(2,1)S(1)} all-to-all(bf16[8,630,32]{1,2,0:T(8,128)(2,1)S(1)} %copy.33), channel_id=1, replica_groups=mesh['grp'=16,'core'=2,'chan'=8] {'chan'}, dimensions={0} | all-to-all | bytes 645120 | tf_op jit(solution)/shard_map/all_to_all | solution.py:29
  27.5 0.2 copy.34
  27.7 4.0 %all_to_all.11 = bf16[2,4,630,32]{2,1,3,0:T(4,128)(2,1)S(1)} all-to-all(bf16[2,4,630,32]{2,1,3,0:T(4,128)(2,1)S(1)} %copy.34), channel_id=1, replica_groups=mesh['grp'=16,'core'=2,'chan'=8] {'core'}, dimensions={0} | all-to-all | bytes 645120 | tf_op jit(solution)/shard_map/all_to_all | solution.py:31
  31.7 0.8 copy.35
  32.5 0.0 all-gather.5.cloned.1.call-update
  32.5 0.0 all-gather.7.cloned.1.call-start
  32.5 119.2 %all-gather.5.cloned.1.call-done = bf16[32,4,630,32]{2,3,1,0:T(8,128)(2,1)} async-done(((bf16[2,4,630,32]{2,3,1,0:T(8,128)(2,1)}), bf16[32,4,630,32]{2,3,1,0:T(8,128)(2,1)}) %all-gather.5.cloned.1.call-update) | async-done | bytes 5160976 | tf_op jit(solution)/shard_map/all_gather | solution.py:32
  151.8 0.0 all-gather.7.cloned.1.call-update
  151.8 0.0 copy-done
  151.8 34.2 %all_gather.19 = bf16[256,256]{0,1:T(8,128)(2,1)S(1)} all-gather(bf16[256,32]{0,1:T(8,128)(2,1)S(1)} %copy-done), channel_id=1, replica_groups=mesh['grp'=16,'core'=2,'chan'=8] {'chan'}, dimensions={1}, use_global_device_ids=true | all-gather | bytes 147456 | tf_op jit(solution)/shard_map/all_gather | solution.py:20
  186.0 0.0 all-gather.7.cloned.1.call-done
  186.0 13.8 %fusion.1 = f32[16,2,630,256,1,1]{3,2,5,0,1,4:T(8,128)} fusion(bf16[256,2,4,32,1,1]{0,3,2,4,5,1:T(8,128)(2,1)S(1)} %bitcast.33, bf16[2,16,2,4,630,32]{4,5,3,2,1,0:T(8,128)(2,1)} %bitcast.34), kind=kOutput, calls=%fused_computation.2 | convolution fusion | flops 2642411520 | bytes 31096832 | tf_op jit(solution)/shard_map/hgrkpc,qhkc->pgrq/dot_general | solution.py:35
  199.8 12.8 %fusion = bf16[16,2,630,256]{3,2,1,0:T(8,128)(2,1)} fusion(f32[16,2,630,256,1,1]{3,2,5,0,1,4:T(8,128)} %fusion.1), kind=kLoop, calls=%fused_computation.1 | loop fusion | flops 10321920 | bytes 30965760 | tf_op jit(solution)/shard_map/convert_element_type | solution.py:36
  212.6 10.5 %copy.36 = bf16[32,630,256]{2,0,1:T(8,128)(2,1)} copy(bf16[32,630,256]{2,1,0:T(8,128)(2,1)} %bitcast.26) | data formatting | bytes 20643840 | tf_op jit(solution)/shard_map/transpose | solution.py:38
  (2 shorter events, 0.1 us)
Async XLA Ops:
  6.5 145.3 %copy-start = (bf16[256,32]{0,1:T(8,128)(2,1)S(1)}, bf16[256,32]{0,1:T(8,128)(2,1)}, u32[]{:S(2)}) copy-start(bf16[256,32]{0,1:T(8,128)(2,1)} %param.2) | copy-start | bytes 49156
  6.5 145.2 %all-gather.5.cloned.1.call-start = ((), (), s32[]{:S(2)}) async-start(), calls=%async_computation.2 | async-start | bytes 5570560 | tf_op jit(solution)/shard_map/all_gather | solution.py:32
  32.5 153.5 %all-gather.7.cloned.1.call-start = ((), (), s32[]{:S(2)}) async-start(), calls=%async_computation.3 | async-start | bytes 15728640 | tf_op jit(solution)/shard_map/all_gather | solution.py:33
Sparse Core Ops, SparseCore 0:
  32.6 119.1 all-gather.4
  153.6 28.8 all-gather.6

commit v3 on v1

--- a/solution.py
+++ b/solution.py
@@ -1,6 +1,10 @@
+import functools
+
 import jax
 import jax.numpy as jnp
 from jax import lax
+from jax.experimental import pallas as pl
+from jax.experimental.pallas import tpu as pltpu
 from jax.sharding import PartitionSpec as P
 
 
@@ -16,20 +20,49 @@
     return joined.astype(jnp.bfloat16)
 
 
+def correlate_kernel(factor, x_ref, f_ref, o_ref):
+    for s in range(x_ref.shape[0]):
+        acc = lax.dot_general(
+            x_ref[s], f_ref[...], (((1,), (1,)), ((), ())), preferred_element_type=jnp.float32
+        )
+        o_ref[:, s, :] = (acc * factor).astype(o_ref.dtype)
+
+
+def correlate(gathered, queries, factor, strips_per_step=16, rows_per_step=128):
+    strips, share, chans = gathered.shape
+    width = queries.shape[0]
+    grid = (pl.cdiv(share, rows_per_step), strips // strips_per_step)
+    return pl.pallas_call(
+        functools.partial(correlate_kernel, factor),
+        out_shape=jax.ShapeDtypeStruct((share, strips, width), jnp.bfloat16),
+        grid=grid,
+        in_specs=[
+            pl.BlockSpec((strips_per_step, rows_per_step, chans), lambda i, j: (j, i, 0)),
+            pl.BlockSpec((width, chans), lambda i, j: (0, 0)),
+        ],
+        out_specs=pl.BlockSpec((rows_per_step, strips_per_step, width), lambda i, j: (i, j, 0)),
+        cost_estimate=pl.CostEstimate(
+            flops=2 * strips * share * chans * width,
+            bytes_accessed=2 * (strips * share * chans + width * chans + strips * share * width),
+            transcendentals=0,
+        ),
+    )(gathered, queries)
+
+
 def local(frame_one, frame_two):
     queries = lax.all_gather(frame_one, "chan", axis=1, tiled=True)
     channels = queries.shape[1]
-    factor = 1.0 / jnp.sqrt(jnp.float32(channels))
+    factor = 1.0 / float(channels) ** 0.5
     pooled = pool_strip(frame_two)
     groups = lax.axis_size("chan")
     share = pooled.shape[0] // groups
     slices = pooled.shape[1]
     blocks = pooled.reshape(groups, share, slices)
     traded = lax.all_to_all(blocks, "chan", split_axis=0, concat_axis=0, tiled=True)
+    traded = jnp.transpose(traded, (1, 0, 2)).reshape(share, groups * slices)
     gathered = lax.all_gather(traded, "rows", axis=0, tiled=False)
-    split_queries = queries.reshape(queries.shape[0], groups, slices)
-    values = jnp.einsum("skpc,qkc->psq", gathered, split_queries, preferred_element_type=jnp.float32)
-    values = (values * factor).astype(jnp.bfloat16)
+    strips = gathered.shape[0]
+    values = correlate(gathered, queries, factor)
     return jnp.transpose(values, (1, 0, 2))
 
 

time: 132 us -> 130 us (0.985)
  Pallas kernels: 0 us -> 18.2 us
  matrix products: 10.7 us -> 0 us
  local copies, waits for them, and re-layouts: 14 us -> 5.18 us
    pallas_call x0 -> x1, Pallas kernels: none -> 18.2 us  [correlate(): pl.pallas_call(functools.partial(correlate_kernel, factor), out_shape=jax...]
    dot_general x1 -> x0, matrix products: 10.7 us -> none  [local(): jnp.einsum('skpc,qkc->psq', gathered, split_queries, preferred_element_ty...]
    convert_element_type x1 -> x0, local copies, waits for them, and re-layouts: 10.5 us -> none  [local(): values = (values * factor).astype(jnp.bfloat16)]
  transfers between devices with their start and end apart: 1 -> 1, of which waited for: 1 -> 1; matrix products, arithmetic and copies ran while one was open for 0% -> 1% of each run, Pallas kernels for 0% -> 0%
where the time goes in v3:
time: 130 us; the launch traced here: 128 us
  blocking collectives  50 us (38%)
  waiting for transfers between devices  38.8 us (30%)
  Pallas kernels  18.2 us (14%)
  between operations  13.5 us (10%)
  local copies, waits for them, and re-layouts  5.18 us (4%)
  other arithmetic  2.08 us (2%)
    all_gather x1, waiting for transfers between devices, local(): gathered = lax.all_gather(traded, 'rows', axis=0, tiled=False)  38.8 us
    all_gather x1, blocking collectives, local(): queries = lax.all_gather(frame_one, 'chan', axis=1, tiled=True)  34.7 us
    pallas_call x1, Pallas kernels, correlate(): pl.pallas_call(functools.partial(correlate_kernel, factor), out_shape=jax...  18.2 us
    all_to_all x1, blocking collectives, local(): lax.all_to_all(blocks, 'chan', split_axis=0, concat_axis=0, tiled=True)  15.3 us
  transfers between devices with their start and end apart: 1, of which 1 were waited for; matrix products, arithmetic and copies ran while one was open for 1% of the time, Pallas kernels for 0%

profile of v3, /device:TPU:8, one launch (start us, length us, event | category | flops | bytes accessed | tf_op | source)
XLA Modules:
  0.0 127.8 jit_solution(18182261713901663760)
XLA Ops:
  6.5 0.0 copy-start
  6.5 0.0 all-gather.2.cloned.1.call-start
  6.5 1.1 copy.15
  7.7 1.3 %copy.16 = f32[8,480,32]{2,1,0:T(8,128)S(1)} copy(bf16[8,480,32]{1,2,0:T(8,128)(2,1)} %param.3) | data formatting | bytes 737280 | tf_op jit(solution)/shard_map/reshape | solution.py:14
  9.0 0.4 reshape.27
  9.3 1.6 %reduce_sum.18 = f32[4,240,32]{2,1,0:T(8,128)S(1)} reduce(f32[4,2,240,2,32]{4,3,2,1,0:T(2,128)S(1)} %bitcast.12, f32[]{:T(128)} %constant.2.clone.1), dimensions={1,3}, to_apply=%region_0.0 | reduce | flops 92160 | bytes 614404 | tf_op jit(solution)/shard_map/reduce_sum | solution.py:14
  10.9 0.1 broadcast_multiply_fusion
  11.0 0.4 reduce_sum.19
  11.4 0.1 copy.18
  11.5 0.1 copy.22
  11.6 0.1 concatenate.4
  11.7 0.4 convert_element_type.6
  12.2 15.3 %all_to_all.5 = bf16[8,630,32]{1,2,0:T(8,128)(2,1)S(1)} all-to-all(bf16[8,630,32]{1,2,0:T(8,128)(2,1)S(1)} %copy.19), channel_id=1, replica_groups=mesh['rows'=32,'chan'=8] {'chan'}, dimensions={0} | all-to-all | bytes 645120 | tf_op jit(solution)/shard_map/all_to_all | solution.py:61
  27.5 0.9 copy.20
  28.4 0.0 all-gather.2.cloned.1.call-update
  28.5 0.0 copy-done
  28.5 34.7 %all_gather.7 = bf16[256,256]{0,1:T(8,128)(2,1)S(1)} all-gather(bf16[256,32]{0,1:T(8,128)(2,1)S(1)} %copy-done), channel_id=1, replica_groups=mesh['rows'=32,'chan'=8] {'chan'}, dimensions={1}, use_global_device_ids=true | all-gather | bytes 147456 | tf_op jit(solution)/shard_map/all_gather | solution.py:53
  63.2 0.8 copy.21.f_ref
  63.9 38.8 %all-gather.2.cloned.1.call-done.x_ref = bf16[32,630,256]{2,1,0:T(8,128)(2,1)} async-done(((bf16[1,630,256]{2,1,0:T(8,128)(2,1)}), bf16[32,630,256]{2,1,0:T(8,128)(2,1)}) %all-gather.2.cloned.1.call-update) | async-done | bytes 10321936 | tf_op jit(solution)/shard_map/all_gather | solution.py:63
  102.8 18.2 %shard_map.28 = bf16[630,32,256]{2,1,0:T(8,128)(2,1)} custom-call(bf16[32,630,256]{2,1,0:T(8,128)(2,1)} %all-gather.2.cloned.1.call-done.x_ref, bf16[256,256]{1,0:T(8,128)(2,1)} %copy.21.f_ref), custom_call_target="tpu_custom_call" | custom-call | flops 2642411520 | bytes 20774912 | tf_op jit(solution)/shard_map/pallas_call | solution.py:35
  (2 shorter events, 0.1 us)
Async XLA Ops:
  6.5 21.9 %copy-start = (bf16[256,32]{0,1:T(8,128)(2,1)S(1)}, bf16[256,32]{0,1:T(8,128)(2,1)}, u32[]{:S(2)}) copy-start(bf16[256,32]{0,1:T(8,128)(2,1)} %param.2) | copy-start | bytes 49156
  6.5 96.2 %all-gather.2.cloned.1.call-start = ((), (), s32[]{:S(2)}) async-start(), calls=%async_computation.1 | async-start | bytes 10678272 | tf_op jit(solution)/shard_map/all_gather | solution.py:63
Sparse Core Ops, SparseCore 0:
  28.6 74.1 all-gather.1

commit v4 on v3

v4 whole, which is shorter than its diff:
```python
import functools

import jax
import jax.numpy as jnp
from jax import lax
from jax.experimental import pallas as pl
from jax.experimental.pallas import tpu as pltpu
from jax.sharding import Mesh, PartitionSpec as P


def pool_strip(strip):
    full = strip.astype(jnp.float32)
    rows_n, cols_n, chans = full.shape
    level_one = full.reshape(rows_n // 2, 2, cols_n // 2, 2, chans).mean(axis=(1, 3))
    level_two = level_one.reshape(rows_n // 4, 2, cols_n // 4, 2, chans).mean(axis=(1, 3))
    joined = jnp.concatenate(
        [full.reshape(-1, chans), level_one.reshape(-1, chans), level_two.reshape(-1, chans)],
        axis=0,
    )
    return joined.astype(jnp.bfloat16)


def correlate_kernel(factor, x_ref, f_ref, o_ref):
    for s in range(x_ref.shape[0]):
        acc = lax.dot_general(
            x_ref[s], f_ref[...], (((1,), (1,)), ((), ())), preferred_element_type=jnp.float32
        )
        o_ref[:, s, :] = (acc * factor).astype(o_ref.dtype)


def correlate(gathered, queries, factor, share, rows_per_step=160):
    halves, strips, half_rows, chans = gathered.shape
    width = queries.shape[0]
    per_half = half_rows // rows_per_step
    grid = (pl.cdiv(share, rows_per_step),)
    return pl.pallas_call(
        functools.partial(correlate_kernel, factor),
        out_shape=jax.ShapeDtypeStruct((share, strips, width), jnp.bfloat16),
        grid=grid,
        in_specs=[
            pl.BlockSpec((None, strips, rows_per_step, chans), lambda i: (i // per_half, 0, i % per_half, 0)),
            pl.BlockSpec((width, chans), lambda i: (0, 0)),
        ],
        out_specs=pl.BlockSpec((rows_per_step, strips, width), lambda i: (i, 0, 0)),
        cost_estimate=pl.CostEstimate(
            flops=2 * strips * share * chans * width,
            bytes_accessed=2 * (strips * share * chans + width * chans + strips * share * width),
            transcendentals=0,
        ),
    )(gathered, queries)


def local(frame_one, frame_two):
    groups = lax.axis_size("chan")
    cores = lax.axis_size("core")
    pieces = lax.all_gather(frame_one, "chan", axis=0, tiled=False)
    queries = jnp.transpose(pieces, (1, 0, 2)).reshape(frame_one.shape[0], -1)
    channels = queries.shape[1]
    factor = 1.0 / float(channels) ** 0.5
    pooled = pool_strip(frame_two)
    share = pooled.shape[0] // groups
    slices = pooled.shape[1]
    blocks = pooled.reshape(groups, share, slices)
    traded = lax.all_to_all(blocks, "chan", split_axis=0, concat_axis=0, tiled=True)
    traded = jnp.transpose(traded, (1, 0, 2)).reshape(share, channels)
    padded_rows = -(-share // (16 * cores)) * 16 * cores
    traded = jnp.pad(traded, ((0, padded_rows - share), (0, 0)))
    halves = traded.reshape(cores, padded_rows // cores, channels)
    mine = lax.all_to_all(halves, "core", split_axis=0, concat_axis=0, tiled=False)
    pair = lax.all_gather(mine, "ylo", axis=0, tiled=False)
    ring = lax.all_gather(pair, "z", axis=0, tiled=False)
    ring = ring.reshape(-1, padded_rows // cores, channels)
    both = lax.all_gather(ring, "core", axis=0, tiled=False)
    values = correlate(both, queries, factor, share)
    return jnp.transpose(values, (1, 0, 2))


def solution(mesh):
    z = 8
    rows = mesh.shape["rows"]
    devices = mesh.devices.reshape(z, rows // (2 * z), 2, mesh.shape["chan"])
    fine = Mesh(devices, ("z", "ylo", "core", "chan"))
    strips = ("z", "ylo", "core")
    in_specs = (P(strips, "chan"), P(strips, None, "chan"))
    out_specs = P(None, "chan", strips)
    return jax.shard_map(local, mesh=fine, in_specs=in_specs, out_specs=out_specs, check_vma=False)
```

time: 130 us -> 170 us (1.31)
  waiting for transfers between devices: 38.8 us -> 64.4 us
  blocking collectives: 50 us -> 64.1 us
  Pallas kernels: 18.2 us -> 20.8 us
    all_gather x1 -> x2, waiting for transfers between devices: 38.8 us -> 64.3 us  [the longest x1 64.3 us: local(): ring = lax.all_gather(pair, 'z', axis=0, tiled=False)]
    all_gather x1 -> x2, blocking collectives: 34.7 us -> 44.7 us  [the longest x1 34.2 us: local(): pieces = lax.all_gather(frame_one, 'chan', axis=0, tiled=False)]
    all_to_all x0 -> x1, blocking collectives: none -> 4 us  [local(): lax.all_to_all(halves, 'core', split_axis=0, concat_axis=0, tiled=False)]
    pallas_call x1, Pallas kernels: 18.2 us -> 20.8 us  [correlate(): pl.pallas_call(functools.partial(correlate_kernel, factor), out_shape=jax...]
  transfers between devices with their start and end apart: 1 -> 2, of which waited for: 1 -> 1; matrix products, arithmetic and copies ran while one was open for 1% -> 0% of each run, Pallas kernels for 0% -> 0%
where the time goes in v4:
time: 170 us; the launch traced here: 169 us
  waiting for transfers between devices  64.4 us (38%)
  blocking collectives  64.1 us (38%)
  Pallas kernels  20.8 us (12%)
  between operations  13.5 us (8%)
  local copies, waits for them, and re-layouts  4.51 us (3%)
  other arithmetic  2.08 us (1%)
    all_gather x1, waiting for transfers between devices, local(): ring = lax.all_gather(pair, 'z', axis=0, tiled=False)  64.3 us
    all_gather x1, blocking collectives, local(): pieces = lax.all_gather(frame_one, 'chan', axis=0, tiled=False)  34.2 us
    pallas_call x1, Pallas kernels, correlate(): pl.pallas_call(functools.partial(correlate_kernel, factor), out_shape=jax...  20.8 us
    all_to_all x1, blocking collectives, local(): lax.all_to_all(blocks, 'chan', split_axis=0, concat_axis=0, tiled=True)  15.3 us
    all_gather x1, blocking collectives, local(): pair = lax.all_gather(mine, 'ylo', axis=0, tiled=False)  10.5 us
    all_to_all x1, blocking collectives, local(): lax.all_to_all(halves, 'core', split_axis=0, concat_axis=0, tiled=False)  4 us
  transfers between devices with their start and end apart: 2, of which 1 were waited for; matrix products, arithmetic and copies ran while one was open for 0% of the time, Pallas kernels for 0%

profile of v4, /device:TPU:8, one launch (start us, length us, event | category | flops | bytes accessed | tf_op | source)
XLA Modules:
  0.0 169.4 jit_solution(3652600418660298844)
XLA Ops:
  6.5 0.0 copy-start
  6.5 0.0 all-gather.8.cloned.1.call-start
  6.5 1.1 copy.16
  7.7 1.3 copy.17
  9.0 0.4 reshape.36
  9.3 1.6 reduce_sum.18
  10.9 0.1 broadcast_multiply_fusion
  11.0 0.4 reduce_sum.19
  11.4 0.1 copy.19
  11.5 0.1 copy.24
  11.6 0.1 concatenate.4
  11.7 0.4 convert_element_type.8
  12.2 15.3 %all_to_all.10 = bf16[8,630,32]{1,2,0:T(8,128)(2,1)S(1)} all-to-all(bf16[8,630,32]{1,2,0:T(8,128)(2,1)S(1)} %copy.20), channel_id=1, replica_groups=mesh['z'=8,'ylo'=2,'core'=2,'chan'=8] {'chan'}, dimensions={0} | all-to-all | bytes 645120 | tf_op jit(solution)/shard_map/all_to_all | solution.py:64
  27.5 0.2 copy.25
  27.8 4.0 %all_to_all.11 = bf16[2,320,256]{2,1,0:T(8,128)(2,1)S(1)} all-to-all(bf16[2,320,256]{2,1,0:T(8,128)(2,1)S(1)} %bitcast.26), channel_id=1, replica_groups=mesh['z'=8,'ylo'=2,'core'=2,'chan'=8] {'core'}, dimensions={0} | all-to-all | bytes 655360 | tf_op jit(solution)/shard_map/all_to_all | solution.py:69
  31.7 10.5 %all-gather = bf16[4,320,256]{2,1,0:T(8,128)(2,1)} all-gather(bf16[2,320,256]{2,1,0:T(8,128)(2,1)S(1)} %all_to_all.11), channel_id=2, replica_groups=mesh['z'=8,'ylo'=2,'core'=2,'chan'=8] {'ylo'}, dimensions={0}, use_global_device_ids=true | all-gather | bytes 983040 | tf_op jit(solution)/shard_map/all_gather | solution.py:70
  42.3 0.0 all-gather.8.cloned.1.call-update
  42.3 0.0 all-gather.6.cloned.1.call-start
  42.4 64.3 %all-gather.8.cloned.1.call-done = bf16[16,2,320,256]{3,2,1,0:T(8,128)(2,1)} async-done(((bf16[2,2,320,256]{3,2,1,0:T(8,128)(2,1)}), bf16[16,2,320,256]{3,2,1,0:T(8,128)(2,1)}) %all-gather.8.cloned.1.call-update) | async-done | bytes 5242896 | tf_op jit(solution)/shard_map/all_gather | solution.py:71
  106.7 0.0 all-gather.6.cloned.1.call-update
  106.7 0.0 copy-done
  106.7 34.2 %all-gather.2 = bf16[2048,32]{0,1:T(8,128)(2,1)S(1)} all-gather(bf16[256,32]{0,1:T(8,128)(2,1)S(1)} %copy-done), channel_id=4, replica_groups=mesh['z'=8,'ylo'=2,'core'=2,'chan'=8] {'chan'}, dimensions={0}, use_global_device_ids=true | all-gather | bytes 147456 | tf_op jit(solution)/shard_map/all_gather | solution.py:56
  141.0 0.7 copy.23.f_ref
  141.8 0.0 all-gather.6.cloned.1.call-done.x_ref
  141.8 20.8 %shard_map.28 = bf16[630,32,256]{2,1,0:T(8,128)(2,1)} custom-call(bf16[2,32,320,256]{3,2,1,0:T(8,128)(2,1)} %all-gather.6.cloned.1.call-done.x_ref, bf16[256,256]{1,0:T(8,128)(2,1)} %copy.23.f_ref), custom_call_target="tpu_custom_call" | custom-call | flops 2642411520 | bytes 20774912 | tf_op jit(solution)/shard_map/pallas_call | solution.py:36
  (5 shorter events, 0.1 us)
Async XLA Ops:
  6.5 100.2 %copy-start = (bf16[256,32]{0,1:T(8,128)(2,1)S(1)}, bf16[256,32]{0,1:T(8,128)(2,1)}, u32[]{:S(2)}) copy-start(bf16[256,32]{0,1:T(8,128)(2,1)} %param.2) | copy-start | bytes 49156
  6.5 100.2 %all-gather.8.cloned.1.call-start = ((), (), s32[]{:S(2)}) async-start(), calls=%async_computation.3 | async-start | bytes 5898240 | tf_op jit(solution)/shard_map/all_gather | solution.py:71
  42.3 99.4 %all-gather.6.cloned.1.call-start = ((), (), s32[]{:S(2)}) async-start(), calls=%async_computation.2 | async-start | bytes 15728640 | tf_op jit(solution)/shard_map/all_gather | solution.py:73
Sparse Core Ops, SparseCore 0:
  42.4 64.2 all-gather.7
  108.5 26.7 all-gather.5

commit v5 on v3

--- a/solution.py
+++ b/solution.py
@@ -6,6 +6,8 @@
 from jax.experimental import pallas as pl
 from jax.experimental.pallas import tpu as pltpu
 from jax.sharding import PartitionSpec as P
+
+MESH_ID = pl.DeviceIdType.MESH
 
 
 def pool_strip(strip):
@@ -18,6 +20,60 @@
         axis=0,
     )
     return joined.astype(jnp.bfloat16)
+
+
+def trade_kernel(n, x_ref, o_ref, buf, send_sem, recv_sem):
+    me = lax.axis_index("chan")
+    row = lax.axis_index("rows")
+    barrier = pltpu.get_barrier_semaphore()
+    for k in range(1, n):
+        peer = lax.rem(me + k, n)
+        pl.semaphore_signal(barrier, inc=1, device_id=(row, peer), device_id_type=MESH_ID)
+    pl.semaphore_wait(barrier, n - 1)
+    sends = []
+    for k in range(1, n):
+        peer = lax.rem(me + k, n)
+        copy = pltpu.make_async_remote_copy(
+            src_ref=x_ref.at[peer],
+            dst_ref=buf.at[me],
+            send_sem=send_sem.at[k],
+            recv_sem=recv_sem.at[k],
+            device_id=(row, peer),
+            device_id_type=MESH_ID,
+        )
+        copy.start()
+        sends.append(copy)
+    o_ref[me] = x_ref[me]
+    for k in range(1, n):
+        source = lax.rem(me + n - k, n)
+        arrival = pltpu.make_async_remote_copy(
+            src_ref=x_ref.at[me],
+            dst_ref=buf.at[source],
+            send_sem=send_sem.at[k],
+            recv_sem=recv_sem.at[k],
+            device_id=(row, source),
+            device_id_type=MESH_ID,
+        )
+        arrival.wait_recv()
+        o_ref[source] = buf[source]
+    for copy in sends:
+        copy.wait_send()
+
+
+def trade(blocks):
+    n = blocks.shape[0]
+    return pl.pallas_call(
+        functools.partial(trade_kernel, n),
+        out_shape=jax.ShapeDtypeStruct(blocks.shape, blocks.dtype),
+        in_specs=[pl.BlockSpec(memory_space=pltpu.VMEM)],
+        out_specs=pl.BlockSpec(memory_space=pltpu.VMEM),
+        scratch_shapes=[
+            pltpu.VMEM(blocks.shape, blocks.dtype),
+            pltpu.SemaphoreType.DMA((n,)),
+            pltpu.SemaphoreType.DMA((n,)),
+        ],
+        compiler_params=pltpu.CompilerParams(collective_id=0, has_side_effects=True),
+    )(blocks)
 
 
 def correlate_kernel(factor, x_ref, f_ref, o_ref):
@@ -57,11 +113,10 @@
     groups = lax.axis_size("chan")
     share = pooled.shape[0] // groups
     slices = pooled.shape[1]
-    blocks = pooled.reshape(groups, share, slices)
-    traded = lax.all_to_all(blocks, "chan", split_axis=0, concat_axis=0, tiled=True)
-    traded = jnp.transpose(traded, (1, 0, 2)).reshape(share, groups * slices)
+    blocks = jnp.transpose(pooled.reshape(groups, share, slices), (0, 2, 1))
+    traded = trade(blocks)
+    traded = jnp.transpose(traded, (2, 0, 1)).reshape(share, channels)
     gathered = lax.all_gather(traded, "rows", axis=0, tiled=False)
-    strips = gathered.shape[0]
     values = correlate(gathered, queries, factor)
     return jnp.transpose(values, (1, 0, 2))
 

time: 130 us -> 131 us (level)
  blocking collectives: 50 us -> 34.5 us
  Pallas kernels: 18.2 us -> 30.2 us
  waiting for transfers between devices: 38.8 us -> 41.5 us
  local copies, waits for them, and re-layouts: 5.18 us -> 6.87 us
    all_to_all x1 -> x0, blocking collectives: 15.3 us -> none  [local(): lax.all_to_all(blocks, 'chan', split_axis=0, concat_axis=0, tiled=True)]
    pallas_call x0 -> x1, Pallas kernels: none -> 12 us  [trade(): pl.pallas_call(functools.partial(trade_kernel, n), out_shape=jax.ShapeDty...]
    all_gather x1, waiting for transfers between devices: 38.8 us -> 41.5 us  [local(): gathered = lax.all_gather(traded, 'rows', axis=0, tiled=False)]
where the time goes in v5:
time: 131 us; the launch traced here: 129 us
  waiting for transfers between devices  41.5 us (32%)
  blocking collectives  34.5 us (26%)
  Pallas kernels  30.2 us (23%)
  between operations  13.5 us (10%)
  local copies, waits for them, and re-layouts  6.87 us (5%)
  other arithmetic  2.08 us (2%)
    all_gather x1, waiting for transfers between devices, local(): gathered = lax.all_gather(traded, 'rows', axis=0, tiled=False)  41.5 us
    all_gather x1, blocking collectives, local(): queries = lax.all_gather(frame_one, 'chan', axis=1, tiled=True)  34.5 us
    pallas_call x1, Pallas kernels, correlate(): pl.pallas_call(functools.partial(correlate_kernel, factor), out_shape=jax...  18.2 us
    pallas_call x1, Pallas kernels, trade(): pl.pallas_call(functools.partial(trade_kernel, n), out_shape=jax.ShapeDty...  12 us
  transfers between devices with their start and end apart: 1, of which 1 were waited for; matrix products, arithmetic and copies ran while one was open for 1% of the time, Pallas kernels for 0%

profile of v5, /device:TPU:8, one launch (start us, length us, event | category | flops | bytes accessed | tf_op | source)
XLA Modules:
  0.0 128.6 jit_solution(6793124379917362416)
XLA Ops:
  6.5 0.0 copy-start
  6.5 0.0 all-gather.2.cloned.1.call-start
  6.5 1.1 copy.16
  7.7 1.3 %copy.17 = f32[8,480,32]{2,1,0:T(8,128)S(1)} copy(bf16[8,480,32]{1,2,0:T(8,128)(2,1)} %param.3) | data formatting | bytes 737280 | tf_op jit(solution)/shard_map/reshape | solution.py:16
  9.0 0.4 reshape.27
  9.3 1.6 %reduce_sum.18 = f32[4,240,32]{2,1,0:T(8,128)S(1)} reduce(f32[4,2,240,2,32]{4,3,2,1,0:T(2,128)S(1)} %bitcast.15, f32[]{:T(128)} %constant.2.clone.1), dimensions={1,3}, to_apply=%region_0.0 | reduce | flops 92160 | bytes 614404 | tf_op jit(solution)/shard_map/reduce_sum | solution.py:16
  10.9 0.1 broadcast_multiply_fusion
  11.0 0.4 reduce_sum.19
  11.4 0.1 copy.19
  11.5 0.1 copy.23
  11.6 0.1 concatenate.4
  11.7 0.4 convert_element_type.6
  12.2 0.8 copy.25
  12.9 12.0 %shard_map.28 = bf16[8,32,630]{2,1,0:T(8,128)(2,1)} custom-call(bf16[8,32,630]{2,1,0:T(8,128)(2,1)} %bitcast.17), custom_call_target="tpu_custom_call" | custom-call | tf_op jit(solution)/shard_map/pallas_call | solution.py:65
  24.9 1.9 %copy.21 = bf16[1,630,256]{2,1,0:T(8,128)(2,1)} copy(bf16[1,630,256]{1,2,0:T(8,128)(2,1)} %bitcast.18) | data formatting | bytes 645120 | tf_op jit(solution)/shard_map/all_gather;reshape | solution.py:119
  26.8 0.0 all-gather.2.cloned.1.call-update
  26.8 0.0 copy-done
  26.8 34.5 %all_gather.7 = bf16[256,256]{0,1:T(8,128)(2,1)S(1)} all-gather(bf16[256,32]{0,1:T(8,128)(2,1)S(1)} %copy-done), channel_id=1, replica_groups=mesh['rows'=32,'chan'=8] {'chan'}, dimensions={1}, use_global_device_ids=true | all-gather | bytes 147456 | tf_op jit(solution)/shard_map/all_gather | solution.py:109
  61.3 0.8 copy.22.f_ref
  62.1 41.5 %all-gather.2.cloned.1.call-done.x_ref = bf16[32,630,256]{2,1,0:T(8,128)(2,1)} async-done(((bf16[1,630,256]{2,1,0:T(8,128)(2,1)}), bf16[32,630,256]{2,1,0:T(8,128)(2,1)}) %all-gather.2.cloned.1.call-update) | async-done | bytes 10321936 | tf_op jit(solution)/shard_map/all_gather | solution.py:119
  103.6 18.2 %shard_map.29 = bf16[630,32,256]{2,1,0:T(8,128)(2,1)} custom-call(bf16[32,630,256]{2,1,0:T(8,128)(2,1)} %all-gather.2.cloned.1.call-done.x_ref, bf16[256,256]{1,0:T(8,128)(2,1)} %copy.22.f_ref), custom_call_target="tpu_custom_call" | custom-call | flops 2642411520 | bytes 20774912 | tf_op jit(solution)/shard_map/pallas_call | solution.py:91
  (1 shorter events, 0.0 us)
Async XLA Ops:
  6.5 20.2 %copy-start = (bf16[256,32]{0,1:T(8,128)(2,1)S(1)}, bf16[256,32]{0,1:T(8,128)(2,1)}, u32[]{:S(2)}) copy-start(bf16[256,32]{0,1:T(8,128)(2,1)} %param.2) | copy-start | bytes 49156
  6.5 97.0 %all-gather.2.cloned.1.call-start = ((), (), s32[]{:S(2)}) async-start(), calls=%async_computation | async-start | bytes 10678272 | tf_op jit(solution)/shard_map/all_gather | solution.py:119
Sparse Core Ops, SparseCore 0:
  26.9 76.6 all-gather.1

commit v6 on v5

--- a/solution.py
+++ b/solution.py
@@ -78,15 +78,13 @@
 
 def correlate_kernel(factor, x_ref, f_ref, o_ref):
     for s in range(x_ref.shape[0]):
-        acc = lax.dot_general(
-            x_ref[s], f_ref[...], (((1,), (1,)), ((), ())), preferred_element_type=jnp.float32
-        )
+        acc = jnp.dot(x_ref[s], f_ref[...], preferred_element_type=jnp.float32)
         o_ref[:, s, :] = (acc * factor).astype(o_ref.dtype)
 
 
-def correlate(gathered, queries, factor, strips_per_step=16, rows_per_step=128):
+def correlate(gathered, queries, factor, strips_per_step=32, rows_per_step=128):
     strips, share, chans = gathered.shape
-    width = queries.shape[0]
+    width = queries.shape[1]
     grid = (pl.cdiv(share, rows_per_step), strips // strips_per_step)
     return pl.pallas_call(
         functools.partial(correlate_kernel, factor),
@@ -94,7 +92,7 @@
         grid=grid,
         in_specs=[
             pl.BlockSpec((strips_per_step, rows_per_step, chans), lambda i, j: (j, i, 0)),
-            pl.BlockSpec((width, chans), lambda i, j: (0, 0)),
+            pl.BlockSpec((chans, width), lambda i, j: (0, 0)),
         ],
         out_specs=pl.BlockSpec((rows_per_step, strips_per_step, width), lambda i, j: (i, j, 0)),
         cost_estimate=pl.CostEstimate(
@@ -117,7 +115,7 @@
     traded = trade(blocks)
     traded = jnp.transpose(traded, (2, 0, 1)).reshape(share, channels)
     gathered = lax.all_gather(traded, "rows", axis=0, tiled=False)
-    values = correlate(gathered, queries, factor)
+    values = correlate(gathered, queries.T, factor)
     return jnp.transpose(values, (1, 0, 2))
 
 

time: 131 us -> 133 us (1.015)
  Pallas kernels: 30.2 us -> 32.1 us
  blocking collectives: 34.5 us -> 36.3 us
    pallas_call x1, Pallas kernels: 18.2 us -> 20.1 us  [correlate(): pl.pallas_call(functools.partial(correlate_kernel, factor), out_shape=jax...]
    all_gather x1, blocking collectives: 34.5 us -> 36.3 us  [local(): queries = lax.all_gather(frame_one, 'chan', axis=1, tiled=True)]
  transfers between devices with their start and end apart: 1 -> 1, of which waited for: 1 -> 1; matrix products, arithmetic and copies ran while one was open for 1% -> 0% of each run, Pallas kernels for 0% -> 0%
where the time goes in v6:
time: 133 us; the launch traced here: 131 us
  waiting for transfers between devices  40.7 us (31%)
  blocking collectives  36.3 us (27%)
  Pallas kernels  32.1 us (24%)
  between operations  13.5 us (10%)
  local copies, waits for them, and re-layouts  6.11 us (5%)
  other arithmetic  2.08 us (2%)
    all_gather x1, waiting for transfers between devices, local(): gathered = lax.all_gather(traded, 'rows', axis=0, tiled=False)  40.7 us
    all_gather x1, blocking collectives, local(): queries = lax.all_gather(frame_one, 'chan', axis=1, tiled=True)  36.3 us
    pallas_call x1, Pallas kernels, correlate(): pl.pallas_call(functools.partial(correlate_kernel, factor), out_shape=jax...  20.1 us
    pallas_call x1, Pallas kernels, trade(): pl.pallas_call(functools.partial(trade_kernel, n), out_shape=jax.ShapeDty...  12 us
  transfers between devices with their start and end apart: 1, of which 1 were waited for; matrix products, arithmetic and copies ran while one was open for 0% of the time, Pallas kernels for 0%

profile of v6, /device:TPU:8, one launch (start us, length us, event | category | flops | bytes accessed | tf_op | source)
XLA Modules:
  0.0 130.7 jit_solution(5934215012055661839)
XLA Ops:
  6.5 0.0 copy-start
  6.5 0.0 all-gather.2.cloned.1.call-start
  6.5 1.1 copy.13
  7.7 1.3 copy.14
  9.0 0.4 reshape.27
  9.3 1.6 %reduce_sum.18 = f32[4,240,32]{2,1,0:T(8,128)S(1)} reduce(f32[4,2,240,2,32]{4,3,2,1,0:T(2,128)S(1)} %bitcast.16, f32[]{:T(128)} %constant.2.clone.1), dimensions={1,3}, to_apply=%region_0.0 | reduce | flops 92160 | bytes 614404 | tf_op jit(solution)/shard_map/reduce_sum | solution.py:16
  10.9 0.1 broadcast_multiply_fusion
  11.0 0.4 reduce_sum.19
  11.4 0.1 copy.16
  11.5 0.1 copy.19
  11.6 0.1 concatenate.4
  11.7 0.4 convert_element_type.6
  12.2 0.8 copy.21
  12.9 12.0 %shard_map.28 = bf16[8,32,630]{2,1,0:T(8,128)(2,1)} custom-call(bf16[8,32,630]{2,1,0:T(8,128)(2,1)} %bitcast.18), custom_call_target="tpu_custom_call" | custom-call | tf_op jit(solution)/shard_map/pallas_call | solution.py:65
  24.9 1.9 %copy.18 = bf16[1,630,256]{2,1,0:T(8,128)(2,1)} copy(bf16[1,630,256]{1,2,0:T(8,128)(2,1)} %bitcast.19) | data formatting | bytes 645120 | tf_op jit(solution)/shard_map/all_gather;reshape | solution.py:117
  26.8 0.0 all-gather.2.cloned.1.call-update
  26.8 0.0 copy-done
  26.8 36.3 %all_gather.7 = bf16[256,256]{0,1:T(8,128)(2,1)} all-gather(bf16[256,32]{0,1:T(8,128)(2,1)S(1)} %copy-done), channel_id=1, replica_groups=mesh['rows'=32,'chan'=8] {'chan'}, dimensions={1}, use_global_device_ids=true | all-gather | bytes 147456 | tf_op jit(solution)/shard_map/all_gather | solution.py:107
  63.1 40.7 %all-gather.2.cloned.1.call-done.x_ref = bf16[32,630,256]{2,1,0:T(8,128)(2,1)} async-done(((bf16[1,630,256]{2,1,0:T(8,128)(2,1)}), bf16[32,630,256]{2,1,0:T(8,128)(2,1)}) %all-gather.2.cloned.1.call-update) | async-done | bytes 10321936 | tf_op jit(solution)/shard_map/all_gather | solution.py:117
  103.8 20.1 %shard_map.29 = bf16[630,32,256]{2,1,0:T(8,128)(2,1)} custom-call(bf16[32,630,256]{2,1,0:T(8,128)(2,1)} %all-gather.2.cloned.1.call-done.x_ref, bf16[256,256]{1,0:T(8,128)(2,1)} %bitcast.21), custom_call_target="tpu_custom_call" | custom-call | flops 2642411520 | bytes 20774912 | tf_op jit(solution)/shard_map/pallas_call | solution.py:89
  (1 shorter events, 0.0 us)
Async XLA Ops:
  6.5 20.2 %copy-start = (bf16[256,32]{0,1:T(8,128)(2,1)S(1)}, bf16[256,32]{0,1:T(8,128)(2,1)}, u32[]{:S(2)}) copy-start(bf16[256,32]{0,1:T(8,128)(2,1)} %param.2) | copy-start | bytes 49156
  6.5 97.2 %all-gather.2.cloned.1.call-start = ((), (), s32[]{:S(2)}) async-start(), calls=%async_computation | async-start | bytes 10678272 | tf_op jit(solution)/shard_map/all_gather | solution.py:117
Sparse Core Ops, SparseCore 0:
  26.9 76.8 all-gather.1

commit v7 on v6

--- a/solution.py
+++ b/solution.py
@@ -76,31 +76,42 @@
     )(blocks)
 
 
-def correlate_kernel(factor, x_ref, f_ref, o_ref):
+def correlate_kernel(factor, x_ref, f_ref, *refs):
+    o_ref = refs[-1]
     for s in range(x_ref.shape[0]):
         acc = jnp.dot(x_ref[s], f_ref[...], preferred_element_type=jnp.float32)
         o_ref[:, s, :] = (acc * factor).astype(o_ref.dtype)
 
 
-def correlate(gathered, queries, factor, strips_per_step=32, rows_per_step=128):
-    strips, share, chans = gathered.shape
+def correlate(gathered, queries, factor, share, first, earlier=None, strips_per_step=16, rows_per_step=160):
+    strips, rows, chans = gathered.shape
     width = queries.shape[1]
-    grid = (pl.cdiv(share, rows_per_step), strips // strips_per_step)
+    row_steps = rows // rows_per_step
+    grid = (row_steps, strips // strips_per_step)
+    in_specs = [
+        pl.BlockSpec((strips_per_step, rows_per_step, chans), lambda i, j: (j, i, 0)),
+        pl.BlockSpec((chans, width), lambda i, j: (0, 0)),
+    ]
+    operands = [gathered, queries]
+    aliases = {}
+    if earlier is not None:
+        in_specs.append(pl.BlockSpec(memory_space=pl.ANY))
+        operands.append(earlier)
+        aliases = {2: 0}
+    offset = first // rows_per_step
     return pl.pallas_call(
         functools.partial(correlate_kernel, factor),
         out_shape=jax.ShapeDtypeStruct((share, strips, width), jnp.bfloat16),
         grid=grid,
-        in_specs=[
-            pl.BlockSpec((strips_per_step, rows_per_step, chans), lambda i, j: (j, i, 0)),
-            pl.BlockSpec((chans, width), lambda i, j: (0, 0)),
-        ],
-        out_specs=pl.BlockSpec((rows_per_step, strips_per_step, width), lambda i, j: (i, j, 0)),
+        in_specs=in_specs,
+        out_specs=pl.BlockSpec((rows_per_step, strips_per_step, width), lambda i, j: (i + offset, j, 0)),
+        input_output_aliases=aliases,
         cost_estimate=pl.CostEstimate(
-            flops=2 * strips * share * chans * width,
-            bytes_accessed=2 * (strips * share * chans + width * chans + strips * share * width),
+            flops=2 * strips * rows * chans * width,
+            bytes_accessed=2 * (strips * rows * chans + width * chans + strips * rows * width),
             transcendentals=0,
         ),
-    )(gathered, queries)
+    )(*operands)
 
 
 def local(frame_one, frame_two):
@@ -114,8 +125,15 @@
     blocks = jnp.transpose(pooled.reshape(groups, share, slices), (0, 2, 1))
     traded = trade(blocks)
     traded = jnp.transpose(traded, (2, 0, 1)).reshape(share, channels)
-    gathered = lax.all_gather(traded, "rows", axis=0, tiled=False)
-    values = correlate(gathered, queries.T, factor)
+    chunks = 2
+    chunk_rows = -(-share // (160 * chunks)) * 160
+    traded = jnp.pad(traded, ((0, chunk_rows * chunks - share), (0, 0)))
+    weights = queries.T
+    values = None
+    for c in range(chunks):
+        piece = traded[c * chunk_rows:(c + 1) * chunk_rows]
+        gathered = lax.all_gather(piece, "rows", axis=0, tiled=False)
+        values = correlate(gathered, weights, factor, share, c * chunk_rows, values)
     return jnp.transpose(values, (1, 0, 2))
 
 

time: 133 us -> 186 us (1.40)
  waiting for transfers between devices: 40.7 us -> 92.7 us
    all_gather x1 -> x2, waiting for transfers between devices: 40.7 us -> 92.6 us  [local(): gathered = lax.all_gather(piece, 'rows', axis=0, tiled=False)]
    another operation x1 -> x0, local copies, waits for them, and re-layouts: 1.87 us -> none  [local(): gathered = lax.all_gather(traded, 'rows', axis=0, tiled=False)]
    pallas_call x1 -> x2, Pallas kernels: 20.1 us -> 19.5 us  [correlate(): pl.pallas_call(functools.partial(correlate_kernel, factor), out_shape=jax...]
  transfers between devices with their start and end apart: 1 -> 2, of which waited for: 1 -> 2; matrix products, arithmetic and copies ran while one was open for 0% -> 1% of each run, Pallas kernels for 0% -> 5%
where the time goes in v7:
time: 186 us; the launch traced here: 184 us
  waiting for transfers between devices  92.7 us (50%)
  blocking collectives  36.2 us (19%)
  Pallas kernels  31.5 us (17%)
  between operations  13.5 us (7%)
  local copies, waits for them, and re-layouts  7.82 us (4%)
  other arithmetic  2.08 us (1%)
    all_gather x2, waiting for transfers between devices, local(): gathered = lax.all_gather(piece, 'rows', axis=0, tiled=False)  92.6 us
    all_gather x1, blocking collectives, local(): queries = lax.all_gather(frame_one, 'chan', axis=1, tiled=True)  36.2 us
    pallas_call x2, Pallas kernels, correlate(): pl.pallas_call(functools.partial(correlate_kernel, factor), out_shape=jax...  19.5 us
    pallas_call x1, Pallas kernels, trade(): pl.pallas_call(functools.partial(trade_kernel, n), out_shape=jax.ShapeDty...  12 us
  transfers between devices with their start and end apart: 2, of which 2 were waited for; matrix products, arithmetic and copies ran while one was open for 1% of the time, Pallas kernels for 5%

profile of v7, /device:TPU:8, one launch (start us, length us, event | category | flops | bytes accessed | tf_op | source)
XLA Modules:
  0.0 183.8 jit_solution(8310909172896613840)
XLA Ops:
  6.5 0.0 all-gather.4.cloned.1.call-start
  6.5 1.1 copy.17
  7.6 1.3 copy.18
  8.9 0.0 copy-start
  8.9 0.4 reshape.32
  9.3 1.6 reduce_sum.18
  10.9 0.1 broadcast_multiply_fusion
  11.0 0.4 reduce_sum.19
  11.4 0.1 copy.20
  11.5 0.1 copy.24
  11.6 0.1 concatenate.4
  11.7 0.4 convert_element_type.8
  12.2 0.8 copy.26
  12.9 12.0 %shard_map.28 = bf16[8,32,630]{2,1,0:T(8,128)(2,1)} custom-call(bf16[8,32,630]{2,1,0:T(8,128)(2,1)} %bitcast.23), custom_call_target="tpu_custom_call" | custom-call | tf_op jit(solution)/shard_map/pallas_call | solution.py:65
  24.9 0.9 slice.10
  25.9 0.8 copy.23
  26.7 0.0 all-gather.4.cloned.1.call-update
  26.7 0.0 all-gather.6.cloned.1.call-start
  26.7 1.1 copy.22
  27.9 0.7 pad_slice_fusion
  28.6 0.0 all-gather.6.cloned.1.call-update
  28.6 0.0 copy-done
  28.6 36.2 %all_gather.17 = bf16[256,256]{0,1:T(8,128)(2,1)} all-gather(bf16[256,32]{0,1:T(8,128)(2,1)S(1)} %copy-done), channel_id=1, replica_groups=mesh['rows'=32,'chan'=8] {'chan'}, dimensions={1}, use_global_device_ids=true | all-gather | bytes 147456 | tf_op jit(solution)/shard_map/all_gather | solution.py:118
  64.8 32.5 %all-gather.4.cloned.1.call-done.x_ref = bf16[32,320,256]{2,1,0:T(8,128)(2,1)} async-done(((bf16[1,320,256]{2,1,0:T(8,128)(2,1)}), bf16[32,320,256]{2,1,0:T(8,128)(2,1)}) %all-gather.4.cloned.1.call-update) | async-done | bytes 5242896 | tf_op jit(solution)/shard_map/all_gather | solution.py:135
  97.3 9.8 %shard_map.29.refs_0_ = bf16[630,32,256]{2,1,0:T(8,128)(2,1)} custom-call(bf16[32,320,256]{2,1,0:T(8,128)(2,1)} %all-gather.4.cloned.1.call-done.x_ref, bf16[256,256]{1,0:T(8,128)(2,1)} %bitcast.24), custom_call_target="tpu_custom_call" | custom-call | flops 1342177280 | bytes 10616832 | tf_op jit(solution)/shard_map/pallas_call | solution.py:102
  107.1 60.2 %all-gather.6.cloned.1.call-done = bf16[10240,256]{1,0:T(8,128)(2,1)} async-done(((bf16[320,256]{1,0:T(8,128)(2,1)}), bf16[10240,256]{1,0:T(8,128)(2,1)}) %all-gather.6.cloned.1.call-update) | async-done | bytes 5242896 | tf_op jit(solution)/shard_map/all_gather | solution.py:135
  167.2 9.8 %shard_map.30 = bf16[630,32,256]{2,1,0:T(8,128)(2,1)} custom-call(bf16[32,320,256]{2,1,0:T(8,128)(2,1)} %bitcast.19, bf16[256,256]{1,0:T(8,128)(2,1)} %bitcast.25, bf16[630,32,256]{2,1,0:T(8,128)(2,1)} %shard_map.29.refs_0_), custom_call_target="tpu_custom_call", output_to_operand_aliasing={{}: (2, {})} | custom-call | flops 1342177280 | bytes 10616832 | tf_op jit(solution)/shard_map/pallas_call | solution.py:102
  (1 shorter events, 0.0 us)
Async XLA Ops:
  6.5 90.7 %all-gather.4.cloned.1.call-start = ((), (), s32[]{:S(2)}) async-start(), calls=%async_computation | async-start | bytes 5406720 | tf_op jit(solution)/shard_map/all_gather | solution.py:135
  8.9 19.7 %copy-start = (bf16[256,32]{0,1:T(8,128)(2,1)S(1)}, bf16[256,32]{0,1:T(8,128)(2,1)}, u32[]{:S(2)}) copy-start(bf16[256,32]{0,1:T(8,128)(2,1)} %param.2) | copy-start | bytes 49156
  26.7 140.6 %all-gather.6.cloned.1.call-start = ((), (), s32[]{:S(2)}) async-start(), calls=%async_computation.1 | async-start | bytes 5406720 | tf_op jit(solution)/shard_map/all_gather | solution.py:135
Sparse Core Ops, SparseCore 0:
  26.8 70.4 all-gather.3
  99.1 68.0 all-gather.5

commit v8 on v6

--- a/solution.py
+++ b/solution.py
@@ -76,22 +76,143 @@
     )(blocks)
 
 
+def gather_kernel(zn, piece_ref, out_ref, send_sem, recv_sem, local_sem):
+    row = lax.axis_index("rows")
+    col = lax.axis_index("chan")
+    b = row % 2
+    ylo = (row // 2) % 2
+    z = row // 4
+    m = ylo * 2 + b
+    other = 1 - ylo
+
+    def device(zz, yy, cc):
+        return (((zz % zn) * 2 + yy) * 2 + cc, col)
+
+    partner = device(z, ylo, 1 - b)
+    ups = device(z + 1, ylo, b)
+    downs = device(z + zn - 1, ylo, b)
+    side = [device(z, other, c) for c in range(2)]
+
+    barrier = pltpu.get_barrier_semaphore()
+    for peer in [partner, ups, downs] + side:
+        pl.semaphore_signal(barrier, inc=1, device_id=peer, device_id_type=MESH_ID)
+    pl.semaphore_wait(barrier, 5)
+
+    def remote(src, dst, idx, peer, arrival=None):
+        arrival = idx if arrival is None else arrival
+        return pltpu.make_async_remote_copy(
+            src_ref=src, dst_ref=dst, send_sem=send_sem.at[idx], recv_sem=recv_sem.at[arrival],
+            device_id=peer, device_id_type=MESH_ID,
+        )
+
+    started = []
+
+    def send(src, dst, idx, peer, arrival=None):
+        copy = remote(src, dst, idx, peer, arrival)
+        copy.start()
+        started.append(copy)
+
+    def arrive(dst, idx):
+        remote(dst, dst, idx, partner).wait_recv()
+
+    own = []
+    for h in range(2):
+        copy = pltpu.make_async_copy(piece_ref.at[h], out_ref.at[h, z, m], local_sem.at[h])
+        copy.start()
+        own.append(copy)
+    for h in range(2):
+        send(piece_ref.at[h], out_ref.at[h, z, m], h, partner)
+    for c in range(2):
+        send(piece_ref.at[c], out_ref.at[c, z, m], 2 + c, side[c], 4 + b)
+    for copy in own:
+        copy.wait()
+    arrive(out_ref.at[b, z, ylo * 2 + 1 - b], b)
+    arrive(out_ref.at[1 - b, z, ylo * 2 + 1 - b], 1 - b)
+    side_slots = pl.ds(other * 2, 2)
+    for c in range(2):
+        arrive(out_ref.at[b, z, other * 2 + c], 4 + c)
+    send(out_ref.at[b, z, side_slots], out_ref.at[b, z, side_slots], 14, partner)
+
+    steps = zn // 2
+    for t in range(1, steps + 1):
+        up_block = (z - (t - 1) + zn) % zn
+        down_block = (z + (t - 1)) % zn
+        if t < steps:
+            up_src = out_ref.at[b, up_block]
+            down_src = out_ref.at[b, down_block]
+        else:
+            up_src = out_ref.at[b, up_block, pl.ds(0, 2)]
+            down_src = out_ref.at[b, down_block, pl.ds(2, 2)]
+        send(up_src, up_src, 6 + (t - 1), ups)
+        send(down_src, down_src, 10 + (t - 1), downs)
+        got_up = (z - t + zn) % zn
+        got_down = (z + t) % zn
+        if t < steps:
+            up_dst = out_ref.at[b, got_up]
+            down_dst = out_ref.at[b, got_down]
+        else:
+            up_dst = out_ref.at[b, got_up, pl.ds(0, 2)]
+            down_dst = out_ref.at[b, got_down, pl.ds(2, 2)]
+        arrive(up_dst, 6 + (t - 1))
+        send(up_dst, up_dst, 15 + (t - 1), partner)
+        arrive(down_dst, 10 + (t - 1))
+        send(down_dst, down_dst, 19 + (t - 1), partner)
+
+    arrive(out_ref.at[1 - b, z, side_slots], 14)
+    for t in range(1, steps + 1):
+        got_up = (z - t + zn) % zn
+        got_down = (z + t) % zn
+        if t < steps:
+            up_dst = out_ref.at[1 - b, got_up]
+            down_dst = out_ref.at[1 - b, got_down]
+        else:
+            up_dst = out_ref.at[1 - b, got_up, pl.ds(0, 2)]
+            down_dst = out_ref.at[1 - b, got_down, pl.ds(2, 2)]
+        arrive(up_dst, 15 + (t - 1))
+        arrive(down_dst, 19 + (t - 1))
+    for copy in started:
+        copy.wait_send()
+
+
+def gather(piece, strips):
+    halves, rows, chans = piece.shape
+    zn = strips // 4
+    sems = 23
+    out = pl.pallas_call(
+        functools.partial(gather_kernel, zn),
+        out_shape=jax.ShapeDtypeStruct((halves, zn, 4, rows, chans), piece.dtype),
+        in_specs=[pl.BlockSpec(memory_space=pl.ANY)],
+        out_specs=pl.BlockSpec(memory_space=pl.ANY),
+        scratch_shapes=[
+            pltpu.SemaphoreType.DMA((sems,)),
+            pltpu.SemaphoreType.DMA((sems,)),
+            pltpu.SemaphoreType.DMA((2,)),
+        ],
+        compiler_params=pltpu.CompilerParams(collective_id=1, has_side_effects=True),
+    )(piece)
+    return out.reshape(halves, strips, rows, chans)
+
+
 def correlate_kernel(factor, x_ref, f_ref, o_ref):
     for s in range(x_ref.shape[0]):
         acc = jnp.dot(x_ref[s], f_ref[...], preferred_element_type=jnp.float32)
         o_ref[:, s, :] = (acc * factor).astype(o_ref.dtype)
 
 
-def correlate(gathered, queries, factor, strips_per_step=32, rows_per_step=128):
-    strips, share, chans = gathered.shape
+def correlate(gathered, queries, factor, share, strips_per_step=16, rows_per_step=160):
+    halves, strips, half_rows, chans = gathered.shape
     width = queries.shape[1]
+    per_half = half_rows // rows_per_step
     grid = (pl.cdiv(share, rows_per_step), strips // strips_per_step)
     return pl.pallas_call(
         functools.partial(correlate_kernel, factor),
         out_shape=jax.ShapeDtypeStruct((share, strips, width), jnp.bfloat16),
         grid=grid,
         in_specs=[
-            pl.BlockSpec((strips_per_step, rows_per_step, chans), lambda i, j: (j, i, 0)),
+            pl.BlockSpec(
+                (None, strips_per_step, rows_per_step, chans),
+                lambda i, j: (i // per_half, j, i % per_half, 0),
+            ),
             pl.BlockSpec((chans, width), lambda i, j: (0, 0)),
         ],
         out_specs=pl.BlockSpec((rows_per_step, strips_per_step, width), lambda i, j: (i, j, 0)),
@@ -109,13 +230,16 @@
     factor = 1.0 / float(channels) ** 0.5
     pooled = pool_strip(frame_two)
     groups = lax.axis_size("chan")
+    strips = lax.axis_size("rows")
     share = pooled.shape[0] // groups
     slices = pooled.shape[1]
     blocks = jnp.transpose(pooled.reshape(groups, share, slices), (0, 2, 1))
     traded = trade(blocks)
     traded = jnp.transpose(traded, (2, 0, 1)).reshape(share, channels)
-    gathered = lax.all_gather(traded, "rows", axis=0, tiled=False)
-    values = correlate(gathered, queries.T, factor)
+    padded = -(-share // 320) * 320
+    traded = jnp.pad(traded, ((0, padded - share), (0, 0)))
+    gathered = gather(traded.reshape(2, padded // 2, channels), strips)
+    values = correlate(gathered, queries.T, factor, share)
     return jnp.transpose(values, (1, 0, 2))
 
 

time: 133 us -> 151 us (1.14)
  Pallas kernels: 32.1 us -> 104 us
  waiting for transfers between devices: 40.7 us -> 0 us
  between operations: 13.5 us -> 0.08 us
    pallas_call x0 -> x1, Pallas kernels: none -> 76 us  [gather(): pl.pallas_call(functools.partial(gather_kernel, zn), out_shape=jax.ShapeD...]
    all_gather x1 -> x0, waiting for transfers between devices: 40.7 us -> none  [local(): gathered = lax.all_gather(traded, 'rows', axis=0, tiled=False)]
    pallas_call x1, Pallas kernels: 20.1 us -> 17.3 us  [correlate(): pl.pallas_call(functools.partial(correlate_kernel, factor), out_shape=jax...]
    another operation x1 -> x0, local copies, waits for them, and re-layouts: 1.87 us -> none  [local(): gathered = lax.all_gather(traded, 'rows', axis=0, tiled=False)]
  transfers between devices with their start and end apart: 1 -> 0, of which waited for: 1 -> 0; matrix products, arithmetic and copies ran while one was open for 0% -> 0% of each run, Pallas kernels for 0% -> 0%
where the time goes in v8:
time: 151 us; the launch traced here: 149 us
  Pallas kernels  104 us (69%)
  blocking collectives  36.4 us (24%)
  local copies, waits for them, and re-layouts  6.12 us (4%)
  other arithmetic  2.08 us (1%)
    pallas_call x1, Pallas kernels, gather(): pl.pallas_call(functools.partial(gather_kernel, zn), out_shape=jax.ShapeD...  76 us
    all_gather x1, blocking collectives, local(): queries = lax.all_gather(frame_one, 'chan', axis=1, tiled=True)  36.4 us
    pallas_call x1, Pallas kernels, correlate(): pl.pallas_call(functools.partial(correlate_kernel, factor), out_shape=jax...  17.3 us
    pallas_call x1, Pallas kernels, trade(): pl.pallas_call(functools.partial(trade_kernel, n), out_shape=jax.ShapeDty...  10.6 us

profile of v8, /device:TPU:8, one launch (start us, length us, event | category | flops | bytes accessed | tf_op | source)
XLA Modules:
  0.0 148.7 jit_solution(6801189623353171378)
XLA Ops:
  0.0 36.4 %all_gather.3 = bf16[256,256]{0,1:T(8,128)(2,1)} all-gather(bf16[256,32]{0,1:T(8,128)(2,1)} %param.2), channel_id=1, replica_groups=mesh['rows'=32,'chan'=8] {'chan'}, dimensions={1}, use_global_device_ids=true | all-gather | bytes 147456 | tf_op jit(solution)/shard_map/all_gather | solution.py:228
  36.4 1.1 copy.13
  37.5 0.3 reshape.36
  37.9 1.3 copy.14
  39.2 1.6 %reduce_sum.18 = f32[4,240,32]{2,1,0:T(8,128)S(1)} reduce(f32[4,2,240,2,32]{4,3,2,1,0:T(2,128)S(1)} %bitcast.19, f32[]{:T(128)} %constant.3.clone.1), dimensions={1,3}, to_apply=%region_0.0 | reduce | flops 92160 | bytes 614404 | tf_op jit(solution)/shard_map/reduce_sum | solution.py:16
  40.8 0.1 broadcast_multiply_fusion
  40.9 0.4 reduce_sum.19
  41.3 0.1 copy.16
  41.4 0.1 copy.19
  41.5 0.1 concatenate.4
  41.6 0.4 convert_element_type.8
  42.0 0.8 copy.21
  42.8 10.6 %shard_map.28 = bf16[8,32,630]{2,1,0:T(8,128)(2,1)} custom-call(bf16[8,32,630]{2,1,0:T(8,128)(2,1)} %bitcast.21), custom_call_target="tpu_custom_call" | custom-call | tf_op jit(solution)/shard_map/pallas_call | solution.py:65
  53.5 1.1 copy.18
  54.6 0.7 pad.4
  55.4 76.0 %shard_map.29 = bf16[2,8,4,320,256]{4,3,2,1,0:T(8,128)(2,1)} custom-call(bf16[2,320,256]{2,1,0:T(8,128)(2,1)} %bitcast.23), custom_call_target="tpu_custom_call" | custom-call | tf_op jit(solution)/shard_map/pallas_call | solution.py:181
  131.4 17.3 %shard_map.30 = bf16[630,32,256]{2,1,0:T(8,128)(2,1)} custom-call(bf16[2,32,320,256]{3,2,1,0:T(8,128)(2,1)} %bitcast.18, bf16[256,256]{1,0:T(8,128)(2,1)} %bitcast.25), custom_call_target="tpu_custom_call" | custom-call | flops 2642411520 | bytes 20774912 | tf_op jit(solution)/shard_map/pallas_call | solution.py:207
  (1 shorter events, 0.0 us)

commit v9 on v8

--- a/solution.py
+++ b/solution.py
@@ -22,7 +22,7 @@
     return joined.astype(jnp.bfloat16)
 
 
-def trade_kernel(n, x_ref, o_ref, buf, send_sem, recv_sem):
+def trade_kernel(n, x_ref, f_ref, o_ref, g_ref, buf, fbuf, send_sem, recv_sem, fsend_sem, frecv_sem):
     me = lax.axis_index("chan")
     row = lax.axis_index("rows")
     barrier = pltpu.get_barrier_semaphore()
@@ -33,47 +33,57 @@
     sends = []
     for k in range(1, n):
         peer = lax.rem(me + k, n)
-        copy = pltpu.make_async_remote_copy(
-            src_ref=x_ref.at[peer],
-            dst_ref=buf.at[me],
-            send_sem=send_sem.at[k],
-            recv_sem=recv_sem.at[k],
-            device_id=(row, peer),
-            device_id_type=MESH_ID,
-        )
-        copy.start()
-        sends.append(copy)
+        for src, dst, ssem, rsem in ((x_ref.at[peer], buf.at[me], send_sem, recv_sem), (f_ref, fbuf.at[me], fsend_sem, frecv_sem)):
+            copy = pltpu.make_async_remote_copy(
+                src_ref=src,
+                dst_ref=dst,
+                send_sem=ssem.at[k],
+                recv_sem=rsem.at[k],
+                device_id=(row, peer),
+                device_id_type=MESH_ID,
+            )
+            copy.start()
+            sends.append(copy)
     o_ref[me] = x_ref[me]
+    g_ref[me] = f_ref[...]
     for k in range(1, n):
         source = lax.rem(me + n - k, n)
-        arrival = pltpu.make_async_remote_copy(
-            src_ref=x_ref.at[me],
-            dst_ref=buf.at[source],
-            send_sem=send_sem.at[k],
-            recv_sem=recv_sem.at[k],
-            device_id=(row, source),
-            device_id_type=MESH_ID,
-        )
-        arrival.wait_recv()
-        o_ref[source] = buf[source]
+        for src, dst, ssem, rsem, out in ((x_ref.at[me], buf.at[source], send_sem, recv_sem, o_ref), (f_ref, fbuf.at[source], fsend_sem, frecv_sem, g_ref)):
+            arrival = pltpu.make_async_remote_copy(
+                src_ref=src,
+                dst_ref=dst,
+                send_sem=ssem.at[k],
+                recv_sem=rsem.at[k],
+                device_id=(row, source),
+                device_id_type=MESH_ID,
+            )
+            arrival.wait_recv()
+            out[source] = dst[...]
     for copy in sends:
         copy.wait_send()
 
 
-def trade(blocks):
+def trade(blocks, piece):
     n = blocks.shape[0]
+    gathered = (n,) + piece.shape
     return pl.pallas_call(
         functools.partial(trade_kernel, n),
-        out_shape=jax.ShapeDtypeStruct(blocks.shape, blocks.dtype),
-        in_specs=[pl.BlockSpec(memory_space=pltpu.VMEM)],
-        out_specs=pl.BlockSpec(memory_space=pltpu.VMEM),
+        out_shape=(
+            jax.ShapeDtypeStruct(blocks.shape, blocks.dtype),
+            jax.ShapeDtypeStruct(gathered, piece.dtype),
+        ),
+        in_specs=[pl.BlockSpec(memory_space=pltpu.VMEM)] * 2,
+        out_specs=(pl.BlockSpec(memory_space=pltpu.VMEM),) * 2,
         scratch_shapes=[
             pltpu.VMEM(blocks.shape, blocks.dtype),
+            pltpu.VMEM(gathered, piece.dtype),
+            pltpu.SemaphoreType.DMA((n,)),
+            pltpu.SemaphoreType.DMA((n,)),
             pltpu.SemaphoreType.DMA((n,)),
             pltpu.SemaphoreType.DMA((n,)),
         ],
         compiler_params=pltpu.CompilerParams(collective_id=0, has_side_effects=True),
-    )(blocks)
+    )(blocks, piece)
 
 
 def gather_kernel(zn, piece_ref, out_ref, send_sem, recv_sem, local_sem):
@@ -225,21 +235,21 @@
 
 
 def local(frame_one, frame_two):
-    queries = lax.all_gather(frame_one, "chan", axis=1, tiled=True)
-    channels = queries.shape[1]
-    factor = 1.0 / float(channels) ** 0.5
     pooled = pool_strip(frame_two)
     groups = lax.axis_size("chan")
+    channels = groups * frame_one.shape[1]
+    factor = 1.0 / float(channels) ** 0.5
     strips = lax.axis_size("rows")
     share = pooled.shape[0] // groups
     slices = pooled.shape[1]
     blocks = jnp.transpose(pooled.reshape(groups, share, slices), (0, 2, 1))
-    traded = trade(blocks)
+    traded, pieces = trade(blocks, frame_one.T)
+    weights = pieces.reshape(channels, frame_one.shape[0])
     traded = jnp.transpose(traded, (2, 0, 1)).reshape(share, channels)
     padded = -(-share // 320) * 320
     traded = jnp.pad(traded, ((0, padded - share), (0, 0)))
     gathered = gather(traded.reshape(2, padded // 2, channels), strips)
-    values = correlate(gathered, queries.T, factor, share)
+    values = correlate(gathered, weights, factor, share)
     return jnp.transpose(values, (1, 0, 2))
 
 

time: 151 us -> 117 us (0.77)
  the two profiles are of different devices: /device:TPU:8 before, /device:TPU:1 now
where the time goes in v9:
time: 117 us
  Pallas kernels  108 us (92%)
  local copies, waits for them, and re-layouts  6.12 us (5%)
  other arithmetic  2.08 us (2%)
    pallas_call x1, Pallas kernels, gather(): pl.pallas_call(functools.partial(gather_kernel, zn), out_shape=jax.ShapeD...  77.7 us
    pallas_call x1, Pallas kernels, correlate(): pl.pallas_call(functools.partial(correlate_kernel, factor), out_shape=jax...  17.3 us
    pallas_call x1, Pallas kernels, trade(): pl.pallas_call(functools.partial(trade_kernel, n), out_shape=(jax.ShapeDt...  13.4 us

profile of v9, /device:TPU:1, one launch (start us, length us, event | category | flops | bytes accessed | tf_op | source)
XLA Modules:
  0.0 116.7 jit_solution(9958986488136059652)
XLA Ops:
  0.0 1.1 copy.13
  1.1 0.4 reshape.39
  1.5 1.3 %copy.14 = f32[8,480,32]{2,1,0:T(8,128)S(1)} copy(bf16[8,480,32]{1,2,0:T(8,128)(2,1)} %param.3) | data formatting | bytes 737280 | tf_op jit(solution)/shard_map/reshape | solution.py:16
  2.8 1.6 %reduce_sum.18 = f32[4,240,32]{2,1,0:T(8,128)S(1)} reduce(f32[4,2,240,2,32]{4,3,2,1,0:T(2,128)S(1)} %bitcast.20, f32[]{:T(128)} %constant.3.clone.1), dimensions={1,3}, to_apply=%region_0.0 | reduce | flops 92160 | bytes 614404 | tf_op jit(solution)/shard_map/reduce_sum | solution.py:16
  4.4 0.1 broadcast_multiply_fusion
  4.4 0.4 reduce_sum.19
  4.9 0.1 copy.16
  4.9 0.1 copy.19
  5.1 0.1 concatenate.4
  5.2 0.4 convert_element_type.8
  5.6 0.8 copy.21
  6.4 13.4 %shard_map.28 = (bf16[8,32,630]{2,1,0:T(8,128)(2,1)}, bf16[8,32,256]{2,1,0:T(8,128)(2,1)}) custom-call(bf16[8,32,630]{2,1,0:T(8,128)(2,1)} %bitcast.22, bf16[32,256]{1,0:T(8,128)(2,1)} %bitcast.28), custom_call_target="tpu_custom_call" | custom-call | tf_op jit(solution)/shard_map/pallas_call | solution.py:69
  19.8 1.1 copy.18
  20.9 0.7 pad.4
  21.7 77.7 %shard_map.29 = bf16[2,8,4,320,256]{4,3,2,1,0:T(8,128)(2,1)} custom-call(bf16[2,320,256]{2,1,0:T(8,128)(2,1)} %bitcast.23), custom_call_target="tpu_custom_call" | custom-call | tf_op jit(solution)/shard_map/pallas_call | solution.py:191
  99.4 17.3 %shard_map.30 = bf16[630,32,256]{2,1,0:T(8,128)(2,1)} custom-call(bf16[2,32,320,256]{3,2,1,0:T(8,128)(2,1)} %bitcast.19, bf16[256,256]{1,0:T(8,128)(2,1)} %bitcast.27), custom_call_target="tpu_custom_call" | custom-call | flops 2642411520 | bytes 20774912 | tf_op jit(solution)/shard_map/pallas_call | solution.py:217
  (1 shorter events, 0.0 us)

commit v10 on v9

--- a/solution.py
+++ b/solution.py
@@ -141,45 +141,59 @@
     side_slots = pl.ds(other * 2, 2)
     for c in range(2):
         arrive(out_ref.at[b, z, other * 2 + c], 4 + c)
-    send(out_ref.at[b, z, side_slots], out_ref.at[b, z, side_slots], 14, partner)
+    send(out_ref.at[b, z, side_slots], out_ref.at[b, z, side_slots], 22, partner)
 
     steps = zn // 2
+    rows = piece_ref.shape[1]
+    carried = pl.ds(ylo, 3)
+    lent = 3 * ylo
+    wanted = 3 * other
+    up_rows = pl.ds(0, rows // 2)
+    down_rows = pl.ds(rows // 2, rows // 2)
+    ring_regions = []
     for t in range(1, steps + 1):
         up_block = (z - (t - 1) + zn) % zn
         down_block = (z + (t - 1)) % zn
         if t < steps:
-            up_src = out_ref.at[b, up_block]
-            down_src = out_ref.at[b, down_block]
+            up_src = out_ref.at[b, up_block, carried]
+            down_src = out_ref.at[b, down_block, carried]
         else:
-            up_src = out_ref.at[b, up_block, pl.ds(0, 2)]
-            down_src = out_ref.at[b, down_block, pl.ds(2, 2)]
+            up_src = out_ref.at[b, up_block, carried, up_rows]
+            down_src = out_ref.at[b, down_block, carried, down_rows]
         send(up_src, up_src, 6 + (t - 1), ups)
         send(down_src, down_src, 10 + (t - 1), downs)
         got_up = (z - t + zn) % zn
         got_down = (z + t) % zn
+        picks = [(got_up, 6, 14, 23, 31, up_rows), (got_down, 10, 18, 27, 35, down_rows)]
+        for block, ring_idx, lend_idx, fwd_idx, fwd_lent_idx, part in picks:
+            if t < steps:
+                dst = out_ref.at[b, block, carried]
+                lend = out_ref.at[b, block, lent]
+            else:
+                dst = out_ref.at[b, block, carried, part]
+                lend = out_ref.at[b, block, lent, part]
+            arrive(dst, ring_idx + (t - 1))
+            send(lend, lend, lend_idx + (t - 1), device(z, other, b))
+            send(dst, dst, fwd_idx + (t - 1), partner)
+            ring_regions.append((block, part, ring_idx, lend_idx, fwd_idx, fwd_lent_idx, t))
+    for block, part, ring_idx, lend_idx, fwd_idx, fwd_lent_idx, t in ring_regions:
         if t < steps:
-            up_dst = out_ref.at[b, got_up]
-            down_dst = out_ref.at[b, got_down]
+            got = out_ref.at[b, block, wanted]
         else:
-            up_dst = out_ref.at[b, got_up, pl.ds(0, 2)]
-            down_dst = out_ref.at[b, got_down, pl.ds(2, 2)]
-        arrive(up_dst, 6 + (t - 1))
-        send(up_dst, up_dst, 15 + (t - 1), partner)
-        arrive(down_dst, 10 + (t - 1))
-        send(down_dst, down_dst, 19 + (t - 1), partner)
-
-    arrive(out_ref.at[1 - b, z, side_slots], 14)
-    for t in range(1, steps + 1):
-        got_up = (z - t + zn) % zn
-        got_down = (z + t) % zn
+            got = out_ref.at[b, block, wanted, part]
+        arrive(got, lend_idx + (t - 1))
+        send(got, got, fwd_lent_idx + (t - 1), partner)
+
+    arrive(out_ref.at[1 - b, z, side_slots], 22)
+    for block, part, ring_idx, lend_idx, fwd_idx, fwd_lent_idx, t in ring_regions:
         if t < steps:
-            up_dst = out_ref.at[1 - b, got_up]
-            down_dst = out_ref.at[1 - b, got_down]
+            dst = out_ref.at[1 - b, block, carried]
+            got = out_ref.at[1 - b, block, wanted]
         else:
-            up_dst = out_ref.at[1 - b, got_up, pl.ds(0, 2)]
-            down_dst = out_ref.at[1 - b, got_down, pl.ds(2, 2)]
-        arrive(up_dst, 15 + (t - 1))
-        arrive(down_dst, 19 + (t - 1))
+            dst = out_ref.at[1 - b, block, carried, part]
+            got = out_ref.at[1 - b, block, wanted, part]
+        arrive(dst, fwd_idx + (t - 1))
+        arrive(got, fwd_lent_idx + (t - 1))
     for copy in started:
         copy.wait_send()
 
@@ -187,7 +201,7 @@
 def gather(piece, strips):
     halves, rows, chans = piece.shape
     zn = strips // 4
-    sems = 23
+    sems = 39
     out = pl.pallas_call(
         functools.partial(gather_kernel, zn),
         out_shape=jax.ShapeDtypeStruct((halves, zn, 4, rows, chans), piece.dtype),

time: 117 us -> 109 us (0.932)
  the two profiles are of different devices: /device:TPU:1 before, /device:TPU:8 now
where the time goes in v10:
time: 109 us; the launch traced here: 107 us
  Pallas kernels  99 us (91%)
  local copies, waits for them, and re-layouts  6.12 us (6%)
  other arithmetic  2.08 us (2%)
    pallas_call x1, Pallas kernels, gather(): pl.pallas_call(functools.partial(gather_kernel, zn), out_shape=jax.ShapeD...  68.2 us
    pallas_call x1, Pallas kernels, correlate(): pl.pallas_call(functools.partial(correlate_kernel, factor), out_shape=jax...  17.3 us
    pallas_call x1, Pallas kernels, trade(): pl.pallas_call(functools.partial(trade_kernel, n), out_shape=(jax.ShapeDt...  13.5 us

profile of v10, /device:TPU:8, one launch (start us, length us, event | category | flops | bytes accessed | tf_op | source)
XLA Modules:
  0.0 107.3 jit_solution(1397468676611753305)
XLA Ops:
  0.0 1.1 %copy.13 = bf16[8,480,32]{1,0,2:T(8,128)(2,1)S(1)} copy(bf16[8,480,32]{1,2,0:T(8,128)(2,1)} %param.3) | data formatting | bytes 491520 | tf_op args[1]
  1.1 0.4 reshape.39
  1.5 1.3 %copy.14 = f32[8,480,32]{2,1,0:T(8,128)S(1)} copy(bf16[8,480,32]{1,2,0:T(8,128)(2,1)} %param.3) | data formatting | bytes 737280 | tf_op jit(solution)/shard_map/reshape | solution.py:16
  2.8 1.6 %reduce_sum.18 = f32[4,240,32]{2,1,0:T(8,128)S(1)} reduce(f32[4,2,240,2,32]{4,3,2,1,0:T(2,128)S(1)} %bitcast.20, f32[]{:T(128)} %constant.3.clone.1), dimensions={1,3}, to_apply=%region_0.0 | reduce | flops 92160 | bytes 614404 | tf_op jit(solution)/shard_map/reduce_sum | solution.py:16
  4.4 0.1 broadcast_multiply_fusion
  4.4 0.4 reduce_sum.19
  4.9 0.1 copy.16
  4.9 0.1 copy.19
  5.1 0.1 concatenate.4
  5.2 0.4 convert_element_type.8
  5.6 0.8 copy.21
  6.4 13.5 %shard_map.28 = (bf16[8,32,630]{2,1,0:T(8,128)(2,1)}, bf16[8,32,256]{2,1,0:T(8,128)(2,1)}) custom-call(bf16[8,32,630]{2,1,0:T(8,128)(2,1)} %bitcast.22, bf16[32,256]{1,0:T(8,128)(2,1)} %bitcast.28), custom_call_target="tpu_custom_call" | custom-call | tf_op jit(solution)/shard_map/pallas_call | solution.py:69
  19.8 1.1 %copy.18 = bf16[630,256]{1,0:T(8,128)(2,1)S(1)} copy(bf16[630,256]{0,1:T(8,128)(2,1)} %bitcast.25) | data formatting | bytes 645120 | tf_op jit(solution)/shard_map/reshape | solution.py:262
  21.0 0.7 pad.4
  21.7 68.2 %shard_map.29 = bf16[2,8,4,320,256]{4,3,2,1,0:T(8,128)(2,1)} custom-call(bf16[2,320,256]{2,1,0:T(8,128)(2,1)} %bitcast.23), custom_call_target="tpu_custom_call" | custom-call | tf_op jit(solution)/shard_map/pallas_call | solution.py:205
  90.0 17.3 %shard_map.30 = bf16[630,32,256]{2,1,0:T(8,128)(2,1)} custom-call(bf16[2,32,320,256]{3,2,1,0:T(8,128)(2,1)} %bitcast.19, bf16[256,256]{1,0:T(8,128)(2,1)} %bitcast.27), custom_call_target="tpu_custom_call" | custom-call | flops 2642411520 | bytes 20774912 | tf_op jit(solution)/shard_map/pallas_call | solution.py:231
  (1 shorter events, 0.0 us)

commit v11 on v10

--- a/solution.py
+++ b/solution.py
@@ -217,10 +217,10 @@
     return out.reshape(halves, strips, rows, chans)
 
 
-def correlate_kernel(factor, x_ref, f_ref, o_ref):
+def correlate_kernel(factor, x_ref, f_ref, o_ref, acc_ref):
     for s in range(x_ref.shape[0]):
-        acc = jnp.dot(x_ref[s], f_ref[...], preferred_element_type=jnp.float32)
-        o_ref[:, s, :] = (acc * factor).astype(o_ref.dtype)
+        acc_ref[:, s, :] = jnp.dot(x_ref[s], f_ref[...], preferred_element_type=jnp.float32)
+    o_ref[...] = (acc_ref[...] * factor).astype(o_ref.dtype)
 
 
 def correlate(gathered, queries, factor, share, strips_per_step=16, rows_per_step=160):
@@ -240,6 +240,7 @@
             pl.BlockSpec((chans, width), lambda i, j: (0, 0)),
         ],
         out_specs=pl.BlockSpec((rows_per_step, strips_per_step, width), lambda i, j: (i, j, 0)),
+        scratch_shapes=[pltpu.VMEM((rows_per_step, strips_per_step, width), jnp.float32)],
         cost_estimate=pl.CostEstimate(
             flops=2 * strips * share * chans * width,
             bytes_accessed=2 * (strips * share * chans + width * chans + strips * share * width),

time: 109 us -> 107 us (0.982)
  Pallas kernels: 99 us -> 96.6 us
    pallas_call x1, Pallas kernels: 17.3 us -> 14.9 us  [correlate(): pl.pallas_call(functools.partial(correlate_kernel, factor), out_shape=jax...]
where the time goes in v11:
time: 107 us; the launch traced here: 105 us
  Pallas kernels  96.6 us (90%)
  local copies, waits for them, and re-layouts  6.12 us (6%)
  other arithmetic  2.08 us (2%)
    pallas_call x1, Pallas kernels, gather(): pl.pallas_call(functools.partial(gather_kernel, zn), out_shape=jax.ShapeD...  68.2 us
    pallas_call x1, Pallas kernels, correlate(): pl.pallas_call(functools.partial(correlate_kernel, factor), out_shape=jax...  14.9 us
    pallas_call x1, Pallas kernels, trade(): pl.pallas_call(functools.partial(trade_kernel, n), out_shape=(jax.ShapeDt...  13.5 us

profile of v11, /device:TPU:8, one launch (start us, length us, event | category | flops | bytes accessed | tf_op | source)
XLA Modules:
  0.0 104.9 jit_solution(945499317767604464)
XLA Ops:
  0.0 1.1 %copy.13 = bf16[8,480,32]{1,0,2:T(8,128)(2,1)S(1)} copy(bf16[8,480,32]{1,2,0:T(8,128)(2,1)} %param.3) | data formatting | bytes 491520 | tf_op args[1]
  1.1 0.4 reshape.39
  1.5 1.3 %copy.14 = f32[8,480,32]{2,1,0:T(8,128)S(1)} copy(bf16[8,480,32]{1,2,0:T(8,128)(2,1)} %param.3) | data formatting | bytes 737280 | tf_op jit(solution)/shard_map/reshape | solution.py:16
  2.8 1.6 %reduce_sum.18 = f32[4,240,32]{2,1,0:T(8,128)S(1)} reduce(f32[4,2,240,2,32]{4,3,2,1,0:T(2,128)S(1)} %bitcast.20, f32[]{:T(128)} %constant.3.clone.1), dimensions={1,3}, to_apply=%region_0.0 | reduce | flops 92160 | bytes 614404 | tf_op jit(solution)/shard_map/reduce_sum | solution.py:16
  4.4 0.1 broadcast_multiply_fusion
  4.4 0.4 reduce_sum.19
  4.9 0.1 copy.16
  4.9 0.1 copy.19
  5.1 0.1 concatenate.4
  5.2 0.4 convert_element_type.8
  5.6 0.8 copy.21
  6.4 13.5 %shard_map.28 = (bf16[8,32,630]{2,1,0:T(8,128)(2,1)}, bf16[8,32,256]{2,1,0:T(8,128)(2,1)}) custom-call(bf16[8,32,630]{2,1,0:T(8,128)(2,1)} %bitcast.22, bf16[32,256]{1,0:T(8,128)(2,1)} %bitcast.28), custom_call_target="tpu_custom_call" | custom-call | tf_op jit(solution)/shard_map/pallas_call | solution.py:69
  19.8 1.1 %copy.18 = bf16[630,256]{1,0:T(8,128)(2,1)S(1)} copy(bf16[630,256]{0,1:T(8,128)(2,1)} %bitcast.25) | data formatting | bytes 645120 | tf_op jit(solution)/shard_map/reshape | solution.py:263
  21.0 0.7 pad.4
  21.7 68.2 %shard_map.29 = bf16[2,8,4,320,256]{4,3,2,1,0:T(8,128)(2,1)} custom-call(bf16[2,320,256]{2,1,0:T(8,128)(2,1)} %bitcast.23), custom_call_target="tpu_custom_call" | custom-call | tf_op jit(solution)/shard_map/pallas_call | solution.py:205
  90.0 14.9 %shard_map.30 = bf16[630,32,256]{2,1,0:T(8,128)(2,1)} custom-call(bf16[2,32,320,256]{3,2,1,0:T(8,128)(2,1)} %bitcast.19, bf16[256,256]{1,0:T(8,128)(2,1)} %bitcast.27), custom_call_target="tpu_custom_call" | custom-call | flops 2642411520 | bytes 20774912 | tf_op jit(solution)/shard_map/pallas_call | solution.py:231
  (1 shorter events, 0.0 us)

commit v12 on v11

--- a/solution.py
+++ b/solution.py
@@ -223,7 +223,7 @@
     o_ref[...] = (acc_ref[...] * factor).astype(o_ref.dtype)
 
 
-def correlate(gathered, queries, factor, share, strips_per_step=16, rows_per_step=160):
+def correlate(gathered, queries, factor, share, strips_per_step=16, rows_per_step=320):
     halves, strips, half_rows, chans = gathered.shape
     width = queries.shape[1]
     per_half = half_rows // rows_per_step

time: 107 us -> 105 us (0.981)
  Pallas kernels: 96.6 us -> 95.2 us
    pallas_call x1, Pallas kernels: 14.9 us -> 13.6 us  [correlate(): pl.pallas_call(functools.partial(correlate_kernel, factor), out_shape=jax...]
where the time goes in v12:
time: 105 us; the launch traced here: 104 us
  Pallas kernels  95.2 us (91%)
  local copies, waits for them, and re-layouts  6.12 us (6%)
  other arithmetic  2.08 us (2%)
    pallas_call x1, Pallas kernels, gather(): pl.pallas_call(functools.partial(gather_kernel, zn), out_shape=jax.ShapeD...  68.2 us
    pallas_call x1, Pallas kernels, correlate(): pl.pallas_call(functools.partial(correlate_kernel, factor), out_shape=jax...  13.6 us
    pallas_call x1, Pallas kernels, trade(): pl.pallas_call(functools.partial(trade_kernel, n), out_shape=(jax.ShapeDt...  13.5 us

profile of v12, /device:TPU:8, one launch (start us, length us, event | category | flops | bytes accessed | tf_op | source)
XLA Modules:
  0.0 103.5 jit_solution(8041989525880538721)
XLA Ops:
  0.0 1.1 %copy.13 = bf16[8,480,32]{1,0,2:T(8,128)(2,1)S(1)} copy(bf16[8,480,32]{1,2,0:T(8,128)(2,1)} %param.3) | data formatting | bytes 491520 | tf_op args[1]
  1.1 0.4 reshape.39
  1.5 1.3 %copy.14 = f32[8,480,32]{2,1,0:T(8,128)S(1)} copy(bf16[8,480,32]{1,2,0:T(8,128)(2,1)} %param.3) | data formatting | bytes 737280 | tf_op jit(solution)/shard_map/reshape | solution.py:16
  2.8 1.6 %reduce_sum.18 = f32[4,240,32]{2,1,0:T(8,128)S(1)} reduce(f32[4,2,240,2,32]{4,3,2,1,0:T(2,128)S(1)} %bitcast.20, f32[]{:T(128)} %constant.3.clone.1), dimensions={1,3}, to_apply=%region_0.0 | reduce | flops 92160 | bytes 614404 | tf_op jit(solution)/shard_map/reduce_sum | solution.py:16
  4.4 0.1 broadcast_multiply_fusion
  4.4 0.4 reduce_sum.19
  4.9 0.1 copy.16
  4.9 0.1 copy.19
  5.1 0.1 concatenate.4
  5.2 0.4 convert_element_type.8
  5.6 0.8 copy.21
  6.4 13.5 %shard_map.28 = (bf16[8,32,630]{2,1,0:T(8,128)(2,1)}, bf16[8,32,256]{2,1,0:T(8,128)(2,1)}) custom-call(bf16[8,32,630]{2,1,0:T(8,128)(2,1)} %bitcast.22, bf16[32,256]{1,0:T(8,128)(2,1)} %bitcast.28), custom_call_target="tpu_custom_call" | custom-call | tf_op jit(solution)/shard_map/pallas_call | solution.py:69
  19.8 1.1 %copy.18 = bf16[630,256]{1,0:T(8,128)(2,1)S(1)} copy(bf16[630,256]{0,1:T(8,128)(2,1)} %bitcast.25) | data formatting | bytes 645120 | tf_op jit(solution)/shard_map/reshape | solution.py:263
  21.0 0.7 pad.4
  21.7 68.2 %shard_map.29 = bf16[2,8,4,320,256]{4,3,2,1,0:T(8,128)(2,1)} custom-call(bf16[2,320,256]{2,1,0:T(8,128)(2,1)} %bitcast.23), custom_call_target="tpu_custom_call" | custom-call | tf_op jit(solution)/shard_map/pallas_call | solution.py:205
  90.0 13.6 %shard_map.30 = bf16[630,32,256]{2,1,0:T(8,128)(2,1)} custom-call(bf16[2,32,320,256]{3,2,1,0:T(8,128)(2,1)} %bitcast.19, bf16[256,256]{1,0:T(8,128)(2,1)} %bitcast.27), custom_call_target="tpu_custom_call" | custom-call | flops 2642411520 | bytes 20774912 | tf_op jit(solution)/shard_map/pallas_call | solution.py:231
  (1 shorter events, 0.0 us)

commit v13 on v12

--- a/solution.py
+++ b/solution.py
@@ -205,7 +205,7 @@
     out = pl.pallas_call(
         functools.partial(gather_kernel, zn),
         out_shape=jax.ShapeDtypeStruct((halves, zn, 4, rows, chans), piece.dtype),
-        in_specs=[pl.BlockSpec(memory_space=pl.ANY)],
+        in_specs=[pl.BlockSpec(memory_space=pltpu.VMEM)],
         out_specs=pl.BlockSpec(memory_space=pl.ANY),
         scratch_shapes=[
             pltpu.SemaphoreType.DMA((sems,)),

time: 105 us -> 104 us (level)
  the two profiles are of different devices: /device:TPU:8 before, /device:TPU:1 now
where the time goes in v13:
time: 104 us
  Pallas kernels  95.6 us (92%)
  local copies, waits for them, and re-layouts  6.12 us (6%)
  other arithmetic  2.08 us (2%)
    pallas_call x1, Pallas kernels, gather(): pl.pallas_call(functools.partial(gather_kernel, zn), out_shape=jax.ShapeD...  68.6 us
    pallas_call x1, Pallas kernels, correlate(): pl.pallas_call(functools.partial(correlate_kernel, factor), out_shape=jax...  13.6 us
    pallas_call x1, Pallas kernels, trade(): pl.pallas_call(functools.partial(trade_kernel, n), out_shape=(jax.ShapeDt...  13.4 us

profile of v13, /device:TPU:1, one launch (start us, length us, event | category | flops | bytes accessed | tf_op | source)
XLA Modules:
  0.0 103.9 jit_solution(5665978164287111567)
XLA Ops:
  0.0 1.1 %copy.13 = bf16[8,480,32]{1,0,2:T(8,128)(2,1)S(1)} copy(bf16[8,480,32]{1,2,0:T(8,128)(2,1)} %param.3) | data formatting | bytes 491520 | tf_op args[1]
  1.1 0.4 reshape.39
  1.5 1.3 %copy.14 = f32[8,480,32]{2,1,0:T(8,128)S(1)} copy(bf16[8,480,32]{1,2,0:T(8,128)(2,1)} %param.3) | data formatting | bytes 737280 | tf_op jit(solution)/shard_map/reshape | solution.py:16
  2.8 1.6 %reduce_sum.18 = f32[4,240,32]{2,1,0:T(8,128)S(1)} reduce(f32[4,2,240,2,32]{4,3,2,1,0:T(2,128)S(1)} %bitcast.20, f32[]{:T(128)} %constant.3.clone.1), dimensions={1,3}, to_apply=%region_0.0 | reduce | flops 92160 | bytes 614404 | tf_op jit(solution)/shard_map/reduce_sum | solution.py:16
  4.4 0.1 broadcast_multiply_fusion
  4.4 0.4 reduce_sum.19
  4.9 0.1 copy.16
  4.9 0.1 copy.19
  5.1 0.1 concatenate.4
  5.2 0.4 convert_element_type.8
  5.6 0.8 copy.21
  6.4 13.4 %shard_map.28 = (bf16[8,32,630]{2,1,0:T(8,128)(2,1)}, bf16[8,32,256]{2,1,0:T(8,128)(2,1)}) custom-call(bf16[8,32,630]{2,1,0:T(8,128)(2,1)} %bitcast.22, bf16[32,256]{1,0:T(8,128)(2,1)} %bitcast.28), custom_call_target="tpu_custom_call" | custom-call | tf_op jit(solution)/shard_map/pallas_call | solution.py:69
  19.8 1.1 %copy.18 = bf16[630,256]{1,0:T(8,128)(2,1)S(1)} copy(bf16[630,256]{0,1:T(8,128)(2,1)} %bitcast.25) | data formatting | bytes 645120 | tf_op jit(solution)/shard_map/reshape | solution.py:263
  20.9 0.7 pad.4
  21.7 68.6 %shard_map.29 = bf16[2,8,4,320,256]{4,3,2,1,0:T(8,128)(2,1)} custom-call(bf16[2,320,256]{2,1,0:T(8,128)(2,1)} %bitcast.23), custom_call_target="tpu_custom_call" | custom-call | tf_op jit(solution)/shard_map/pallas_call | solution.py:205
  90.3 13.6 %shard_map.30 = bf16[630,32,256]{2,1,0:T(8,128)(2,1)} custom-call(bf16[2,32,320,256]{3,2,1,0:T(8,128)(2,1)} %bitcast.19, bf16[256,256]{1,0:T(8,128)(2,1)} %bitcast.27), custom_call_target="tpu_custom_call" | custom-call | flops 2642411520 | bytes 20774912 | tf_op jit(solution)/shard_map/pallas_call | solution.py:231
  (1 shorter events, 0.0 us)

commit v14 on v13

--- a/solution.py
+++ b/solution.py
@@ -151,21 +151,27 @@
     up_rows = pl.ds(0, rows // 2)
     down_rows = pl.ds(rows // 2, rows // 2)
     ring_regions = []
+
+    def send_ring(up, t):
+        if up:
+            block = (z - (t - 1) + zn) % zn
+            part, idx, peer = up_rows, 6, ups
+        else:
+            block = (z + (t - 1)) % zn
+            part, idx, peer = down_rows, 10, downs
+        if t < steps:
+            src = out_ref.at[b, block, carried]
+        else:
+            src = out_ref.at[b, block, carried, part]
+        send(src, src, idx + (t - 1), peer)
+
+    send_ring(True, 1)
+    send_ring(False, 1)
     for t in range(1, steps + 1):
-        up_block = (z - (t - 1) + zn) % zn
-        down_block = (z + (t - 1)) % zn
-        if t < steps:
-            up_src = out_ref.at[b, up_block, carried]
-            down_src = out_ref.at[b, down_block, carried]
-        else:
-            up_src = out_ref.at[b, up_block, carried, up_rows]
-            down_src = out_ref.at[b, down_block, carried, down_rows]
-        send(up_src, up_src, 6 + (t - 1), ups)
-        send(down_src, down_src, 10 + (t - 1), downs)
         got_up = (z - t + zn) % zn
         got_down = (z + t) % zn
-        picks = [(got_up, 6, 14, 23, 31, up_rows), (got_down, 10, 18, 27, 35, down_rows)]
-        for block, ring_idx, lend_idx, fwd_idx, fwd_lent_idx, part in picks:
+        picks = [(True, got_up, 6, 14, 23, 31, up_rows), (False, got_down, 10, 18, 27, 35, down_rows)]
+        for up, block, ring_idx, lend_idx, fwd_idx, fwd_lent_idx, part in picks:
             if t < steps:
                 dst = out_ref.at[b, block, carried]
                 lend = out_ref.at[b, block, lent]
@@ -173,6 +179,8 @@
                 dst = out_ref.at[b, block, carried, part]
                 lend = out_ref.at[b, block, lent, part]
             arrive(dst, ring_idx + (t - 1))
+            if t < steps:
+                send_ring(up, t + 1)
             send(lend, lend, lend_idx + (t - 1), device(z, other, b))
             send(dst, dst, fwd_idx + (t - 1), partner)
             ring_regions.append((block, part, ring_idx, lend_idx, fwd_idx, fwd_lent_idx, t))

time: 104 us -> 102 us (0.981)
  the two profiles are of different devices: /device:TPU:1 before, /device:TPU:8 now
where the time goes in v14:
time: 102 us; the launch traced here: 101 us
  Pallas kernels  92.4 us (91%)
  local copies, waits for them, and re-layouts  6.12 us (6%)
  other arithmetic  2.08 us (2%)
    pallas_call x1, Pallas kernels, gather(): pl.pallas_call(functools.partial(gather_kernel, zn), out_shape=jax.ShapeD...  65.4 us
    pallas_call x1, Pallas kernels, correlate(): pl.pallas_call(functools.partial(correlate_kernel, factor), out_shape=jax...  13.6 us
    pallas_call x1, Pallas kernels, trade(): pl.pallas_call(functools.partial(trade_kernel, n), out_shape=(jax.ShapeDt...  13.5 us

profile of v14, /device:TPU:8, one launch (start us, length us, event | category | flops | bytes accessed | tf_op | source)
XLA Modules:
  0.0 100.7 jit_solution(14686943896558623023)
XLA Ops:
  0.0 1.1 %copy.13 = bf16[8,480,32]{1,0,2:T(8,128)(2,1)S(1)} copy(bf16[8,480,32]{1,2,0:T(8,128)(2,1)} %param.3) | data formatting | bytes 491520 | tf_op args[1]
  1.1 0.4 reshape.39
  1.5 1.3 %copy.14 = f32[8,480,32]{2,1,0:T(8,128)S(1)} copy(bf16[8,480,32]{1,2,0:T(8,128)(2,1)} %param.3) | data formatting | bytes 737280 | tf_op jit(solution)/shard_map/reshape | solution.py:16
  2.8 1.6 %reduce_sum.18 = f32[4,240,32]{2,1,0:T(8,128)S(1)} reduce(f32[4,2,240,2,32]{4,3,2,1,0:T(2,128)S(1)} %bitcast.20, f32[]{:T(128)} %constant.3.clone.1), dimensions={1,3}, to_apply=%region_0.0 | reduce | flops 92160 | bytes 614404 | tf_op jit(solution)/shard_map/reduce_sum | solution.py:16
  4.4 0.1 broadcast_multiply_fusion
  4.4 0.4 reduce_sum.19
  4.9 0.1 copy.16
  4.9 0.1 copy.19
  5.1 0.1 concatenate.4
  5.2 0.4 convert_element_type.8
  5.6 0.8 copy.21
  6.4 13.5 %shard_map.28 = (bf16[8,32,630]{2,1,0:T(8,128)(2,1)}, bf16[8,32,256]{2,1,0:T(8,128)(2,1)}) custom-call(bf16[8,32,630]{2,1,0:T(8,128)(2,1)} %bitcast.22, bf16[32,256]{1,0:T(8,128)(2,1)} %bitcast.28), custom_call_target="tpu_custom_call" | custom-call | tf_op jit(solution)/shard_map/pallas_call | solution.py:69
  19.8 1.1 %copy.18 = bf16[630,256]{1,0:T(8,128)(2,1)S(1)} copy(bf16[630,256]{0,1:T(8,128)(2,1)} %bitcast.25) | data formatting | bytes 645120 | tf_op jit(solution)/shard_map/reshape | solution.py:271
  21.0 0.7 pad.4
  21.7 65.4 %shard_map.29 = bf16[2,8,4,320,256]{4,3,2,1,0:T(8,128)(2,1)} custom-call(bf16[2,320,256]{2,1,0:T(8,128)(2,1)} %bitcast.23), custom_call_target="tpu_custom_call" | custom-call | tf_op jit(solution)/shard_map/pallas_call | solution.py:213
  87.2 13.6 %shard_map.30 = bf16[630,32,256]{2,1,0:T(8,128)(2,1)} custom-call(bf16[2,32,320,256]{3,2,1,0:T(8,128)(2,1)} %bitcast.19, bf16[256,256]{1,0:T(8,128)(2,1)} %bitcast.27), custom_call_target="tpu_custom_call" | custom-call | flops 2642411520 | bytes 20774912 | tf_op jit(solution)/shard_map/pallas_call | solution.py:239
  (1 shorter events, 0.0 us)

commit v15 on v14

--- a/solution.py
+++ b/solution.py
@@ -137,11 +137,8 @@
     for copy in own:
         copy.wait()
     arrive(out_ref.at[b, z, ylo * 2 + 1 - b], b)
-    arrive(out_ref.at[1 - b, z, ylo * 2 + 1 - b], 1 - b)
+    arrive(out_ref.at[b, z, other * 2 + ylo], 4 + ylo)
     side_slots = pl.ds(other * 2, 2)
-    for c in range(2):
-        arrive(out_ref.at[b, z, other * 2 + c], 4 + c)
-    send(out_ref.at[b, z, side_slots], out_ref.at[b, z, side_slots], 22, partner)
 
     steps = zn // 2
     rows = piece_ref.shape[1]
@@ -167,6 +164,9 @@
 
     send_ring(True, 1)
     send_ring(False, 1)
+    arrive(out_ref.at[1 - b, z, ylo * 2 + 1 - b], 1 - b)
+    arrive(out_ref.at[b, z, other * 2 + 1 - ylo], 5 - ylo)
+    send(out_ref.at[b, z, side_slots], out_ref.at[b, z, side_slots], 22, partner)
     for t in range(1, steps + 1):
         got_up = (z - t + zn) % zn
         got_down = (z + t) % zn

time: 102 us -> 102 us (level)
  no operation moved by 1% of the time
where the time goes in v15:
time: 102 us; the launch traced here: 100 us
  Pallas kernels  92.1 us (90%)
  local copies, waits for them, and re-layouts  6.12 us (6%)
  other arithmetic  2.08 us (2%)
    pallas_call x1, Pallas kernels, gather(): pl.pallas_call(functools.partial(gather_kernel, zn), out_shape=jax.ShapeD...  65.1 us
    pallas_call x1, Pallas kernels, correlate(): pl.pallas_call(functools.partial(correlate_kernel, factor), out_shape=jax...  13.6 us
    pallas_call x1, Pallas kernels, trade(): pl.pallas_call(functools.partial(trade_kernel, n), out_shape=(jax.ShapeDt...  13.5 us

profile of v15, /device:TPU:8, one launch (start us, length us, event | category | flops | bytes accessed | tf_op | source)
XLA Modules:
  0.0 100.4 jit_solution(6362405069320202189)
XLA Ops:
  0.0 1.1 %copy.13 = bf16[8,480,32]{1,0,2:T(8,128)(2,1)S(1)} copy(bf16[8,480,32]{1,2,0:T(8,128)(2,1)} %param.3) | data formatting | bytes 491520 | tf_op args[1]
  1.1 0.4 reshape.39
  1.5 1.3 %copy.14 = f32[8,480,32]{2,1,0:T(8,128)S(1)} copy(bf16[8,480,32]{1,2,0:T(8,128)(2,1)} %param.3) | data formatting | bytes 737280 | tf_op jit(solution)/shard_map/reshape | solution.py:16
  2.8 1.6 %reduce_sum.18 = f32[4,240,32]{2,1,0:T(8,128)S(1)} reduce(f32[4,2,240,2,32]{4,3,2,1,0:T(2,128)S(1)} %bitcast.20, f32[]{:T(128)} %constant.3.clone.1), dimensions={1,3}, to_apply=%region_0.0 | reduce | flops 92160 | bytes 614404 | tf_op jit(solution)/shard_map/reduce_sum | solution.py:16
  4.4 0.1 broadcast_multiply_fusion
  4.4 0.4 reduce_sum.19
  4.9 0.1 copy.16
  4.9 0.1 copy.19
  5.1 0.1 concatenate.4
  5.2 0.4 convert_element_type.8
  5.6 0.8 copy.21
  6.4 13.5 %shard_map.28 = (bf16[8,32,630]{2,1,0:T(8,128)(2,1)}, bf16[8,32,256]{2,1,0:T(8,128)(2,1)}) custom-call(bf16[8,32,630]{2,1,0:T(8,128)(2,1)} %bitcast.22, bf16[32,256]{1,0:T(8,128)(2,1)} %bitcast.28), custom_call_target="tpu_custom_call" | custom-call | tf_op jit(solution)/shard_map/pallas_call | solution.py:69
  19.8 1.1 %copy.18 = bf16[630,256]{1,0:T(8,128)(2,1)S(1)} copy(bf16[630,256]{0,1:T(8,128)(2,1)} %bitcast.25) | data formatting | bytes 645120 | tf_op jit(solution)/shard_map/reshape | solution.py:271
  21.0 0.7 pad.4
  21.7 65.1 %shard_map.29 = bf16[2,8,4,320,256]{4,3,2,1,0:T(8,128)(2,1)} custom-call(bf16[2,320,256]{2,1,0:T(8,128)(2,1)} %bitcast.23), custom_call_target="tpu_custom_call" | custom-call | tf_op jit(solution)/shard_map/pallas_call | solution.py:213
  86.8 13.6 %shard_map.30 = bf16[630,32,256]{2,1,0:T(8,128)(2,1)} custom-call(bf16[2,32,320,256]{3,2,1,0:T(8,128)(2,1)} %bitcast.19, bf16[256,256]{1,0:T(8,128)(2,1)} %bitcast.27), custom_call_target="tpu_custom_call" | custom-call | flops 2642411520 | bytes 20774912 | tf_op jit(solution)/shard_map/pallas_call | solution.py:239
  (1 shorter events, 0.0 us)

commit v16 on v15

--- a/solution.py
+++ b/solution.py
@@ -231,7 +231,7 @@
     o_ref[...] = (acc_ref[...] * factor).astype(o_ref.dtype)
 
 
-def correlate(gathered, queries, factor, share, strips_per_step=16, rows_per_step=320):
+def correlate(gathered, queries, factor, share, strips_per_step=32, rows_per_step=320):
     halves, strips, half_rows, chans = gathered.shape
     width = queries.shape[1]
     per_half = half_rows // rows_per_step

time: 102 us -> 104 us (1.020)
  Pallas kernels: 92.1 us -> 94.1 us
    pallas_call x1, Pallas kernels: 13.6 us -> 15.5 us  [correlate(): pl.pallas_call(functools.partial(correlate_kernel, factor), out_shape=jax...]
where the time goes in v16:
time: 104 us; the launch traced here: 102 us
  Pallas kernels  94.1 us (90%)
  local copies, waits for them, and re-layouts  6.12 us (6%)
  other arithmetic  2.08 us (2%)
    pallas_call x1, Pallas kernels, gather(): pl.pallas_call(functools.partial(gather_kernel, zn), out_shape=jax.ShapeD...  65.1 us
    pallas_call x1, Pallas kernels, correlate(): pl.pallas_call(functools.partial(correlate_kernel, factor), out_shape=jax...  15.5 us
    pallas_call x1, Pallas kernels, trade(): pl.pallas_call(functools.partial(trade_kernel, n), out_shape=(jax.ShapeDt...  13.5 us

profile of v16, /device:TPU:8, one launch (start us, length us, event | category | flops | bytes accessed | tf_op | source)
XLA Modules:
  0.0 102.4 jit_solution(6003842180977279001)
XLA Ops:
  0.0 1.1 %copy.13 = bf16[8,480,32]{1,0,2:T(8,128)(2,1)S(1)} copy(bf16[8,480,32]{1,2,0:T(8,128)(2,1)} %param.3) | data formatting | bytes 491520 | tf_op args[1]
  1.1 0.4 reshape.39
  1.5 1.3 %copy.14 = f32[8,480,32]{2,1,0:T(8,128)S(1)} copy(bf16[8,480,32]{1,2,0:T(8,128)(2,1)} %param.3) | data formatting | bytes 737280 | tf_op jit(solution)/shard_map/reshape | solution.py:16
  2.8 1.6 %reduce_sum.18 = f32[4,240,32]{2,1,0:T(8,128)S(1)} reduce(f32[4,2,240,2,32]{4,3,2,1,0:T(2,128)S(1)} %bitcast.20, f32[]{:T(128)} %constant.3.clone.1), dimensions={1,3}, to_apply=%region_0.0 | reduce | flops 92160 | bytes 614404 | tf_op jit(solution)/shard_map/reduce_sum | solution.py:16
  4.4 0.1 broadcast_multiply_fusion
  4.4 0.4 reduce_sum.19
  4.9 0.1 copy.16
  4.9 0.1 copy.19
  5.1 0.1 concatenate.4
  5.2 0.4 convert_element_type.8
  5.6 0.8 copy.21
  6.4 13.5 %shard_map.28 = (bf16[8,32,630]{2,1,0:T(8,128)(2,1)}, bf16[8,32,256]{2,1,0:T(8,128)(2,1)}) custom-call(bf16[8,32,630]{2,1,0:T(8,128)(2,1)} %bitcast.22, bf16[32,256]{1,0:T(8,128)(2,1)} %bitcast.28), custom_call_target="tpu_custom_call" | custom-call | tf_op jit(solution)/shard_map/pallas_call | solution.py:69
  19.8 1.1 %copy.18 = bf16[630,256]{1,0:T(8,128)(2,1)S(1)} copy(bf16[630,256]{0,1:T(8,128)(2,1)} %bitcast.25) | data formatting | bytes 645120 | tf_op jit(solution)/shard_map/reshape | solution.py:271
  21.0 0.7 pad.4
  21.7 65.1 %shard_map.29 = bf16[2,8,4,320,256]{4,3,2,1,0:T(8,128)(2,1)} custom-call(bf16[2,320,256]{2,1,0:T(8,128)(2,1)} %bitcast.23), custom_call_target="tpu_custom_call" | custom-call | tf_op jit(solution)/shard_map/pallas_call | solution.py:213
  86.8 15.5 %shard_map.30 = bf16[630,32,256]{2,1,0:T(8,128)(2,1)} custom-call(bf16[2,32,320,256]{3,2,1,0:T(8,128)(2,1)} %bitcast.19, bf16[256,256]{1,0:T(8,128)(2,1)} %bitcast.27), custom_call_target="tpu_custom_call" | custom-call | flops 2642411520 | bytes 20774912 | tf_op jit(solution)/shard_map/pallas_call | solution.py:239
  (1 shorter events, 0.0 us)

commit v17 on v15

--- a/solution.py
+++ b/solution.py
@@ -265,12 +265,12 @@
     strips = lax.axis_size("rows")
     share = pooled.shape[0] // groups
     slices = pooled.shape[1]
+    padded = -(-share // 320) * 320
     blocks = jnp.transpose(pooled.reshape(groups, share, slices), (0, 2, 1))
+    blocks = jnp.pad(blocks, ((0, 0), (0, 0), (0, padded - share)))
     traded, pieces = trade(blocks, frame_one.T)
     weights = pieces.reshape(channels, frame_one.shape[0])
-    traded = jnp.transpose(traded, (2, 0, 1)).reshape(share, channels)
-    padded = -(-share // 320) * 320
-    traded = jnp.pad(traded, ((0, padded - share), (0, 0)))
+    traded = jnp.transpose(traded, (2, 0, 1)).reshape(padded, channels)
     gathered = gather(traded.reshape(2, padded // 2, channels), strips)
     values = correlate(gathered, weights, factor, share)
     return jnp.transpose(values, (1, 0, 2))

time: 102 us -> 102 us (level)
    another operation x0 -> x2, local copies, waits for them, and re-layouts: none -> 2.4 us  [local(): gathered = gather(traded.reshape(2, padded // 2, channels), strips)]
    reshape x1 -> x0, local copies, waits for them, and re-layouts: 1.14 us -> none  [local(): traded = jnp.transpose(traded, (2, 0, 1)).reshape(share, channels)]
where the time goes in v17:
time: 102 us; the launch traced here: 101 us
  Pallas kernels  92.1 us (90%)
  local copies, waits for them, and re-layouts  6.66 us (7%)
  other arithmetic  2.08 us (2%)
    pallas_call x1, Pallas kernels, gather(): pl.pallas_call(functools.partial(gather_kernel, zn), out_shape=jax.ShapeD...  65.1 us
    pallas_call x1, Pallas kernels, correlate(): pl.pallas_call(functools.partial(correlate_kernel, factor), out_shape=jax...  13.6 us
    pallas_call x1, Pallas kernels, trade(): pl.pallas_call(functools.partial(trade_kernel, n), out_shape=(jax.ShapeDt...  13.5 us
    another operation x2, local copies, waits for them, and re-layouts, local(): gathered = gather(traded.reshape(2, padded // 2, channels), strips)  2.4 us

profile of v17, /device:TPU:8, one launch (start us, length us, event | category | flops | bytes accessed | tf_op | source)
XLA Modules:
  0.0 100.9 jit_solution(15376706182467243748)
XLA Ops:
  0.0 1.1 %copy.13 = bf16[8,480,32]{1,0,2:T(8,128)(2,1)S(1)} copy(bf16[8,480,32]{1,2,0:T(8,128)(2,1)} %param.3) | data formatting | bytes 491520 | tf_op args[1]
  1.1 0.4 reshape.33
  1.5 1.3 %copy.14 = f32[8,480,32]{2,1,0:T(8,128)S(1)} copy(bf16[8,480,32]{1,2,0:T(8,128)(2,1)} %param.3) | data formatting | bytes 737280 | tf_op jit(solution)/shard_map/reshape | solution.py:16
  2.8 1.6 %reduce_sum.18 = f32[4,240,32]{2,1,0:T(8,128)S(1)} reduce(f32[4,2,240,2,32]{4,3,2,1,0:T(2,128)S(1)} %bitcast.19, f32[]{:T(128)} %constant.3.clone.1), dimensions={1,3}, to_apply=%region_0.0 | reduce | flops 92160 | bytes 614404 | tf_op jit(solution)/shard_map/reduce_sum | solution.py:16
  4.4 0.1 broadcast_multiply_fusion
  4.4 0.4 reduce_sum.19
  4.9 0.1 copy.16
  4.9 0.1 copy.19
  5.1 0.1 concatenate.4
  5.2 0.4 convert_element_type.8
  5.7 0.8 pad.4.x_ref
  6.4 13.5 %shard_map.28 = (bf16[8,32,640]{2,1,0:T(8,128)(2,1)}, bf16[8,32,256]{2,1,0:T(8,128)(2,1)}) custom-call(bf16[8,32,640]{2,1,0:T(8,128)(2,1)} %pad.4.x_ref, bf16[32,256]{1,0:T(8,128)(2,1)} %bitcast.26), custom_call_target="tpu_custom_call" | custom-call | tf_op jit(solution)/shard_map/pallas_call | solution.py:69
  19.9 1.3 %reshape_reshape.3 = bf16[2,320,256]{1,0,2:T(2,128)(2,1)S(1)} reshape(bf16[640,8,32]{0,2,1:T(8,128)(2,1)} %bitcast.23) | data formatting | bytes 655360 | tf_op jit(solution)/shard_map/reshape;reshape | solution.py:274
  21.2 1.1 %copy.18.piece_ref = bf16[2,320,256]{2,1,0:T(8,128)(2,1)} copy(bf16[2,320,256]{1,0,2:T(2,128)(2,1)S(1)} %reshape_reshape.3) | data formatting | bytes 655360 | tf_op jit(solution)/shard_map/reshape;reshape | solution.py:274
  22.3 65.1 %shard_map.29 = bf16[2,8,4,320,256]{4,3,2,1,0:T(8,128)(2,1)} custom-call(bf16[2,320,256]{2,1,0:T(8,128)(2,1)} %copy.18.piece_ref), custom_call_target="tpu_custom_call" | custom-call | tf_op jit(solution)/shard_map/pallas_call | solution.py:213
  87.4 13.6 %shard_map.30 = bf16[630,32,256]{2,1,0:T(8,128)(2,1)} custom-call(bf16[2,32,320,256]{3,2,1,0:T(8,128)(2,1)} %bitcast.18, bf16[256,256]{1,0:T(8,128)(2,1)} %bitcast.25), custom_call_target="tpu_custom_call" | custom-call | flops 2642411520 | bytes 20774912 | tf_op jit(solution)/shard_map/pallas_call | solution.py:239
  (2 shorter events, 0.1 us)

commit v18 on v17

--- a/solution.py
+++ b/solution.py
@@ -231,7 +231,7 @@
     o_ref[...] = (acc_ref[...] * factor).astype(o_ref.dtype)
 
 
-def correlate(gathered, queries, factor, share, strips_per_step=16, rows_per_step=320):
+def correlate(gathered, queries, factor, share, strips_per_step=8, rows_per_step=320):
     halves, strips, half_rows, chans = gathered.shape
     width = queries.shape[1]
     per_half = half_rows // rows_per_step

time: 102 us -> 103 us (level)
  no operation moved by 1% of the time
where the time goes in v18:
time: 103 us; the launch traced here: 102 us
  Pallas kernels  92.7 us (90%)
  local copies, waits for them, and re-layouts  6.66 us (6%)
  other arithmetic  2.08 us (2%)
    pallas_call x1, Pallas kernels, gather(): pl.pallas_call(functools.partial(gather_kernel, zn), out_shape=jax.ShapeD...  65.1 us
    pallas_call x1, Pallas kernels, correlate(): pl.pallas_call(functools.partial(correlate_kernel, factor), out_shape=jax...  14.2 us
    pallas_call x1, Pallas kernels, trade(): pl.pallas_call(functools.partial(trade_kernel, n), out_shape=(jax.ShapeDt...  13.5 us
    another operation x2, local copies, waits for them, and re-layouts, local(): gathered = gather(traded.reshape(2, padded // 2, channels), strips)  2.4 us

profile of v18, /device:TPU:8, one launch (start us, length us, event | category | flops | bytes accessed | tf_op | source)
XLA Modules:
  0.0 101.5 jit_solution(2567556647190616061)
XLA Ops:
  0.0 1.1 %copy.13 = bf16[8,480,32]{1,0,2:T(8,128)(2,1)S(1)} copy(bf16[8,480,32]{1,2,0:T(8,128)(2,1)} %param.3) | data formatting | bytes 491520 | tf_op args[1]
  1.1 0.4 reshape.33
  1.5 1.3 %copy.14 = f32[8,480,32]{2,1,0:T(8,128)S(1)} copy(bf16[8,480,32]{1,2,0:T(8,128)(2,1)} %param.3) | data formatting | bytes 737280 | tf_op jit(solution)/shard_map/reshape | solution.py:16
  2.8 1.6 %reduce_sum.18 = f32[4,240,32]{2,1,0:T(8,128)S(1)} reduce(f32[4,2,240,2,32]{4,3,2,1,0:T(2,128)S(1)} %bitcast.19, f32[]{:T(128)} %constant.3.clone.1), dimensions={1,3}, to_apply=%region_0.0 | reduce | flops 92160 | bytes 614404 | tf_op jit(solution)/shard_map/reduce_sum | solution.py:16
  4.4 0.1 broadcast_multiply_fusion
  4.4 0.4 reduce_sum.19
  4.9 0.1 copy.16
  4.9 0.1 copy.19
  5.1 0.1 concatenate.4
  5.2 0.4 convert_element_type.8
  5.7 0.8 pad.4.x_ref
  6.4 13.5 %shard_map.28 = (bf16[8,32,640]{2,1,0:T(8,128)(2,1)}, bf16[8,32,256]{2,1,0:T(8,128)(2,1)}) custom-call(bf16[8,32,640]{2,1,0:T(8,128)(2,1)} %pad.4.x_ref, bf16[32,256]{1,0:T(8,128)(2,1)} %bitcast.26), custom_call_target="tpu_custom_call" | custom-call | tf_op jit(solution)/shard_map/pallas_call | solution.py:69
  19.9 1.3 %reshape_reshape.3 = bf16[2,320,256]{1,0,2:T(2,128)(2,1)S(1)} reshape(bf16[640,8,32]{0,2,1:T(8,128)(2,1)} %bitcast.23) | data formatting | bytes 655360 | tf_op jit(solution)/shard_map/reshape;reshape | solution.py:274
  21.2 1.1 %copy.18.piece_ref = bf16[2,320,256]{2,1,0:T(8,128)(2,1)} copy(bf16[2,320,256]{1,0,2:T(2,128)(2,1)S(1)} %reshape_reshape.3) | data formatting | bytes 655360 | tf_op jit(solution)/shard_map/reshape;reshape | solution.py:274
  22.3 65.1 %shard_map.29 = bf16[2,8,4,320,256]{4,3,2,1,0:T(8,128)(2,1)} custom-call(bf16[2,320,256]{2,1,0:T(8,128)(2,1)} %copy.18.piece_ref), custom_call_target="tpu_custom_call" | custom-call | tf_op jit(solution)/shard_map/pallas_call | solution.py:213
  87.4 14.2 %shard_map.30 = bf16[630,32,256]{2,1,0:T(8,128)(2,1)} custom-call(bf16[2,32,320,256]{3,2,1,0:T(8,128)(2,1)} %bitcast.18, bf16[256,256]{1,0:T(8,128)(2,1)} %bitcast.25), custom_call_target="tpu_custom_call" | custom-call | flops 2642411520 | bytes 20774912 | tf_op jit(solution)/shard_map/pallas_call | solution.py:239
  (2 shorter events, 0.1 us)

commit v19 on v17

--- a/solution.py
+++ b/solution.py
@@ -130,10 +130,10 @@
         copy = pltpu.make_async_copy(piece_ref.at[h], out_ref.at[h, z, m], local_sem.at[h])
         copy.start()
         own.append(copy)
+    for c in range(2):
+        send(piece_ref.at[c], out_ref.at[c, z, m], 2 + c, side[c], 4 + b)
     for h in range(2):
         send(piece_ref.at[h], out_ref.at[h, z, m], h, partner)
-    for c in range(2):
-        send(piece_ref.at[c], out_ref.at[c, z, m], 2 + c, side[c], 4 + b)
     for copy in own:
         copy.wait()
     arrive(out_ref.at[b, z, ylo * 2 + 1 - b], b)

time: 102 us -> 102 us (level)
  no operation moved by 1% of the time
where the time goes in v19:
time: 102 us; the launch traced here: 101 us
  Pallas kernels  92.1 us (90%)
  local copies, waits for them, and re-layouts  6.66 us (7%)
  other arithmetic  2.08 us (2%)
    pallas_call x1, Pallas kernels, gather(): pl.pallas_call(functools.partial(gather_kernel, zn), out_shape=jax.ShapeD...  65.1 us
    pallas_call x1, Pallas kernels, correlate(): pl.pallas_call(functools.partial(correlate_kernel, factor), out_shape=jax...  13.6 us
    pallas_call x1, Pallas kernels, trade(): pl.pallas_call(functools.partial(trade_kernel, n), out_shape=(jax.ShapeDt...  13.5 us
    another operation x2, local copies, waits for them, and re-layouts, local(): gathered = gather(traded.reshape(2, padded // 2, channels), strips)  2.4 us

profile of v19, /device:TPU:8, one launch (start us, length us, event | category | flops | bytes accessed | tf_op | source)
XLA Modules:
  0.0 100.9 jit_solution(18098377800565222791)
XLA Ops:
  0.0 1.1 %copy.13 = bf16[8,480,32]{1,0,2:T(8,128)(2,1)S(1)} copy(bf16[8,480,32]{1,2,0:T(8,128)(2,1)} %param.3) | data formatting | bytes 491520 | tf_op args[1]
  1.1 0.4 reshape.33
  1.5 1.3 %copy.14 = f32[8,480,32]{2,1,0:T(8,128)S(1)} copy(bf16[8,480,32]{1,2,0:T(8,128)(2,1)} %param.3) | data formatting | bytes 737280 | tf_op jit(solution)/shard_map/reshape | solution.py:16
  2.8 1.6 %reduce_sum.18 = f32[4,240,32]{2,1,0:T(8,128)S(1)} reduce(f32[4,2,240,2,32]{4,3,2,1,0:T(2,128)S(1)} %bitcast.19, f32[]{:T(128)} %constant.3.clone.1), dimensions={1,3}, to_apply=%region_0.0 | reduce | flops 92160 | bytes 614404 | tf_op jit(solution)/shard_map/reduce_sum | solution.py:16
  4.4 0.1 broadcast_multiply_fusion
  4.4 0.4 reduce_sum.19
  4.9 0.1 copy.16
  4.9 0.1 copy.19
  5.1 0.1 concatenate.4
  5.2 0.4 convert_element_type.8
  5.7 0.8 pad.4.x_ref
  6.4 13.5 %shard_map.28 = (bf16[8,32,640]{2,1,0:T(8,128)(2,1)}, bf16[8,32,256]{2,1,0:T(8,128)(2,1)}) custom-call(bf16[8,32,640]{2,1,0:T(8,128)(2,1)} %pad.4.x_ref, bf16[32,256]{1,0:T(8,128)(2,1)} %bitcast.26), custom_call_target="tpu_custom_call" | custom-call | tf_op jit(solution)/shard_map/pallas_call | solution.py:69
  19.9 1.3 %reshape_reshape.3 = bf16[2,320,256]{1,0,2:T(2,128)(2,1)S(1)} reshape(bf16[640,8,32]{0,2,1:T(8,128)(2,1)} %bitcast.23) | data formatting | bytes 655360 | tf_op jit(solution)/shard_map/reshape;reshape | solution.py:274
  21.2 1.1 %copy.18.piece_ref = bf16[2,320,256]{2,1,0:T(8,128)(2,1)} copy(bf16[2,320,256]{1,0,2:T(2,128)(2,1)S(1)} %reshape_reshape.3) | data formatting | bytes 655360 | tf_op jit(solution)/shard_map/reshape;reshape | solution.py:274
  22.3 65.1 %shard_map.29 = bf16[2,8,4,320,256]{4,3,2,1,0:T(8,128)(2,1)} custom-call(bf16[2,320,256]{2,1,0:T(8,128)(2,1)} %copy.18.piece_ref), custom_call_target="tpu_custom_call" | custom-call | tf_op jit(solution)/shard_map/pallas_call | solution.py:213
  87.4 13.6 %shard_map.30 = bf16[630,32,256]{2,1,0:T(8,128)(2,1)} custom-call(bf16[2,32,320,256]{3,2,1,0:T(8,128)(2,1)} %bitcast.18, bf16[256,256]{1,0:T(8,128)(2,1)} %bitcast.25), custom_call_target="tpu_custom_call" | custom-call | flops 2642411520 | bytes 20774912 | tf_op jit(solution)/shard_map/pallas_call | solution.py:239
  (2 shorter events, 0.1 us)
